TPU v7x, 128 devices: a whole 4x4x4 slice. The times are simulated.
128 devices in a mesh: seq: 16 (over y, z_hi, core), head: 8 (over z_lo, x).
Axes of the slice: x: 4, y: 4, z: 4 (z_hi: 2, z_lo: 2; z = z_hi * 2 + z_lo), core: 2. Of those that a mesh axis runs over, the one named last changes fastest.
Arguments:
- enc_in: bfloat16 [8192, 4, 768], P(('seq', 'head')), may hold values from -6 to 6
- conv_weight: bfloat16 [5, 768, 1536], replicated, may hold values from -0.09375 to 0.09375
- norm_gain: float32 [1536], replicated, may hold values from 0.25 to 1.75
- w_qkv: bfloat16 [3, 1536, 1536], P(None, None, 'head'), may hold values from -0.63788795 to 0.63788795
- w_out: bfloat16 [1536, 1536], P('head'), may hold values from -0.15625 to 0.15625
- grad_out: bfloat16 [4096, 4, 1536], P(('seq', 'head')), may hold values from -6 to 6
Outputs:
- mixed: bfloat16 [4096, 4, 1536], P(('seq', 'head'))
- grad_input: bfloat16 [8192, 4, 768], P(('seq', 'head'))
- grad_w_qkv: float32 [3, 1536, 1536], P(None, None, 'head')
- grad_w_out: float32 [1536, 1536], P('head')
All inputs are finite; a program needn't handle non-finite values.
Results may differ from a plain program's by a relative error of at most 0.024.
Values may be sent and summed in bfloat16 or wider, within the bound.
A program may use at most 256 MiB of HBM per device.

v0:
```python
import jax
import jax.numpy as jnp
from jax import lax
from jax.sharding import PartitionSpec as P

DH = 192
KW = 5


def padded_2(block, sides, width):
    for axis, dim in sides:
        count = lax.axis_size(axis)
        forward = [(i, i + 1) for i in range(count - 1)]
        backward = [(target, source) for source, target in forward]
        low = lax.ppermute(
            lax.slice_in_dim(block, block.shape[dim] - width, None, axis=dim), axis, forward
        )
        high = lax.ppermute(lax.slice_in_dim(block, 0, width, axis=dim), axis, backward)
        block = jnp.concatenate([low, block, high], axis=dim)
    return block


def body(enc_in, conv_weight, norm_gain, w_qkv, w_out, grad_out):
    fine_rows = enc_in.shape[0]
    slab_rows = fine_rows // 2
    seq_count = enc_in.shape[1]
    out_width = conv_weight.shape[2]
    local_width = w_qkv.shape[2]
    local_heads = local_width // DH
    logit_scale = DH ** (-0.5)
    padded = padded_2(enc_in, ((("seq", "head"), 0),), 2)
    convolved = jnp.zeros((fine_rows, seq_count, out_width), jnp.float32)
    for offset in range(KW):
        convolved = convolved + jnp.einsum(
            "tbi,io->tbo",
            padded[offset : offset + fine_rows],
            conv_weight[offset],
            preferred_element_type=jnp.float32,
        )
    activated, gelu_pull = jax.vjp(jax.nn.gelu, convolved)
    skip = jnp.mean(activated.reshape(slab_rows, 2, seq_count, out_width), axis=1).astype(
        jnp.bfloat16
    )
    skip_wide = skip.astype(jnp.float32)
    inv_rms = lax.rsqrt(jnp.mean(skip_wide * skip_wide, axis=-1, keepdims=True) + 1e-06)
    normed = (skip_wide * inv_rms * norm_gain).astype(jnp.bfloat16)
    normed_rows = lax.all_gather(normed, "head", axis=0, tiled=True)
    grad_rows = lax.all_gather(grad_out, "head", axis=0, tiled=True)
    tower_rows = normed_rows.shape[0]
    qkv = jnp.einsum(
        "tbc,ice->itbe", normed_rows, w_qkv, preferred_element_type=jnp.float32
    ).astype(jnp.bfloat16)
    qkv = qkv.reshape(3, tower_rows, seq_count, local_heads, DH)
    query_matrix, key_matrix, value_matrix = (qkv[0], qkv[1], qkv[2])
    key_all, value_all = (
        lax.all_gather(key_matrix, "seq", axis=0, tiled=True),
        lax.all_gather(value_matrix, "seq", axis=0, tiled=True),
    )
    attention_logits = (
        jnp.einsum("qbhd,kbhd->bhqk", query_matrix, key_all, preferred_element_type=jnp.float32)
        * logit_scale
    )
    row_peak = jnp.max(attention_logits, axis=-1, keepdims=True)
    exponent = jnp.exp(attention_logits - row_peak)
    row_total = jnp.sum(exponent, axis=-1, keepdims=True)
    soft_weights = exponent / row_total
    narrow_probabilities = soft_weights.astype(jnp.bfloat16)
    attention_output = jnp.einsum(
        "bhqk,kbhd->qbhd", narrow_probabilities, value_all, preferred_element_type=jnp.float32
    )
    o_narrow = attention_output.reshape(tower_rows, seq_count, local_width).astype(jnp.bfloat16)
    piece = o_narrow
    head_sum = lax.psum_scatter(
        jnp.einsum("tbe,ec->tbc", piece, w_out, preferred_element_type=jnp.float32).astype(
            jnp.bfloat16
        ),
        "head",
        scatter_dimension=0,
        tiled=True,
    ).astype(jnp.float32)
    mixed = (skip_wide + head_sum).astype(jnp.bfloat16)
    part_w_out = jnp.einsum("tbe,tbc->ec", o_narrow, grad_rows, preferred_element_type=jnp.float32)
    d_out = jnp.einsum("tbc,ec->tbe", grad_rows, w_out, preferred_element_type=jnp.float32).astype(
        jnp.bfloat16
    )
    d_out = d_out.reshape(tower_rows, seq_count, local_heads, DH)
    delta = jnp.sum(d_out.astype(jnp.float32) * attention_output, axis=-1)
    probability_gradient = jnp.einsum(
        "qbhd,kbhd->bhqk", d_out, value_all, preferred_element_type=jnp.float32
    )
    d_scores = soft_weights * (probability_gradient - jnp.transpose(delta, (1, 2, 0))[..., None])
    narrow_gradient = d_scores.astype(jnp.bfloat16)
    query_gradient = logit_scale * jnp.einsum(
        "bhqk,kbhd->qbhd", narrow_gradient, key_all, preferred_element_type=jnp.float32
    )
    key_terms = logit_scale * jnp.einsum(
        "bhqk,qbhd->kbhd", narrow_gradient, query_matrix, preferred_element_type=jnp.float32
    )
    value_terms = jnp.einsum(
        "bhqk,qbhd->kbhd", narrow_probabilities, d_out, preferred_element_type=jnp.float32
    )
    d_keys, d_values = (
        lax.psum_scatter(
            key_terms.astype(jnp.bfloat16), "seq", scatter_dimension=0, tiled=True
        ).astype(jnp.float32),
        lax.psum_scatter(
            value_terms.astype(jnp.bfloat16), "seq", scatter_dimension=0, tiled=True
        ).astype(jnp.float32),
    )
    dqkv = (
        jnp.stack([query_gradient, d_keys, d_values])
        .reshape(3, tower_rows, seq_count, local_width)
        .astype(jnp.bfloat16)
    )
    part_w_qkv = jnp.einsum("tbc,itbe->ice", normed_rows, dqkv, preferred_element_type=jnp.float32)
    piece = dqkv
    d_normed = lax.psum_scatter(
        jnp.einsum("itbe,ice->tbc", piece, w_qkv, preferred_element_type=jnp.float32).astype(
            jnp.bfloat16
        ),
        "head",
        scatter_dimension=0,
        tiled=True,
    ).astype(jnp.float32)
    unit_rows = skip_wide * inv_rms
    scaled = d_normed * norm_gain
    d_skip = grad_out.astype(jnp.float32) + inv_rms * (
        scaled - unit_rows * jnp.mean(scaled * unit_rows, axis=-1, keepdims=True)
    )
    d_act = jnp.repeat(d_skip, 2, axis=0) * 0.5
    d_conv = gelu_pull(d_act)[0].astype(jnp.bfloat16)
    d_pad = padded_2(d_conv, ((("seq", "head"), 0),), 2)
    grad_input = jnp.zeros((fine_rows, seq_count, enc_in.shape[2]), jnp.float32)
    for offset in range(KW):
        grad_input = grad_input + jnp.einsum(
            "tbo,io->tbi",
            d_pad[4 - offset : 4 - offset + fine_rows],
            conv_weight[offset],
            preferred_element_type=jnp.float32,
        )
    grad_w_qkv, grad_w_out = (
        lax.psum(part_w_qkv.astype(jnp.bfloat16), "seq").astype(jnp.float32),
        lax.psum(part_w_out.astype(jnp.bfloat16), "seq").astype(jnp.float32),
    )
    return (mixed, grad_input.astype(jnp.bfloat16), grad_w_qkv, grad_w_out)


def solution(mesh):
    return jax.shard_map(
        body,
        mesh=mesh,
        in_specs=(
            P(("seq", "head"), None, None),
            P(),
            P(),
            P(None, None, "head"),
            P("head", None),
            P(("seq", "head"), None, None),
        ),
        out_specs=(
            P(("seq", "head"), None, None),
            P(("seq", "head"), None, None),
            P(None, None, "head"),
            P("head", None),
        ),
        check_vma=False,
    )
```

profile of v0, /device:TPU:1, one launch (start us, length us, event | category | flops | bytes accessed | tf_op | source)
XLA Modules:
  0.0 743.2 jit_solution(13010598031011791318)
XLA Ops:
  7.2 1.2 fusion.140
  8.4 7.1 collective-permute-start.1
  15.6 1.9 collective-permute-start
  17.5 2.6 fusion.33
  20.1 2.4 fusion.26
  22.6 0.1 collective-permute-done
  22.7 2.4 fusion.37
  25.1 2.5 fusion.22
  27.6 4.4 multiply_multiply_fusion.2
  32.0 2.2 reshape.102
  34.3 2.9 reduce_sum.47
  37.2 1.4 fusion.111
  38.6 0.9 fusion.105
  39.6 0.8 copy.15
  40.5 43.8 %all-gather.7.cloned.1.call-done = bf16[256,4,1536]{2,0,1:T(8,128)(2,1)} async-done(((bf16[32,4,1536]{2,0,1:T(8,128)(2,1)}), bf16[256,4,1536]{2,0,1:T(8,128)(2,1)}) %all-gather.7.cloned.1.call-update) | async-done | bytes 3145744 | tf_op jit(solution)/shard_map/all_gather | solution.py:47
  84.3 3.9 fusion.66
  88.2 0.9 fusion.137
  89.2 0.5 all-gather.11.cloned.1.call-update
  89.8 0.2 reduce-scatter.9.cloned.1.call-start
  90.0 40.5 %all-gather.9.cloned.1.call-done = bf16[256,4,1536]{2,0,1:T(8,128)(2,1)} async-done(((bf16[32,4,1536]{2,0,1:T(8,128)(2,1)}), bf16[256,4,1536]{2,0,1:T(8,128)(2,1)}) %all-gather.9.cloned.1.call-update) | async-done | bytes 3145744 | tf_op jit(solution)/shard_map/all_gather | solution.py:48
  130.4 3.9 convolution_convert_fusion.2
  134.4 71.3 %all-gather.13.cloned.1.call-done = bf16[1,4096,4,192]{1,3,0,2:T(8,128)(2,1)} async-done(((bf16[1,256,4,192]{1,3,0,2:T(8,128)(2,1)}), bf16[1,4096,4,192]{1,3,0,2:T(8,128)(2,1)}) %all-gather.13.cloned.1.call-update) | async-done | bytes 6291472 | tf_op jit(solution)/shard_map/all_gather | solution.py:56
  205.6 11.0 %fusion.8 = f32[4,256,4096]{2,1,0:T(8,128)} fusion(bf16[1,4096,4,192]{1,3,0,2:T(8,128)(2,1)} %all-gather.13.cloned.1.call-done, bf16[3,256,4,192]{1,3,0,2:T(8,128)(2,1)S(1)} %fusion.66), kind=kOutput, calls=%fused_computation.13 | convolution fusion | flops 1610612736 | bytes 23461888 | tf_op jit(solution)/shard_map/qbhd,kbhd->bhqk/dot_general | solution.py:60
  216.6 18.3 %fusion.141 = (f32[4,256]{1,0:T(4,128)S(1)}, f32[4,256,4096]{2,1,0:T(8,128)}) fusion(f32[4,256,4096]{2,1,0:T(8,128)} %fusion.8), kind=kOutput, calls=%fused_computation.145 | output fusion | flops 16781312 | bytes 33558528 | tf_op jit(solution)/shard_map/sub | solution.py:64
  234.9 7.5 %fusion.5 = bf16[4,256,4096]{2,1,0:T(8,128)(2,1)S(1)} fusion(f32[4,256,4096]{2,1,0:T(8,128)} %get-tuple-element.25, f32[4,256]{1,0:T(4,128)S(1)} %get-tuple-element.24), kind=kLoop, calls=%fused_computation.8 | loop fusion | flops 8388608 | bytes 25169920 | tf_op jit(solution)/shard_map/convert_element_type | solution.py:67
  242.4 3.2 copy-done.1
  245.7 4.5 fusion.13
  250.2 0.3 reduce-scatter.7.cloned.1.call-start
  250.5 25.8 %all-gather.11.cloned.1.call-done = bf16[1,4096,4,192]{1,3,0,2:T(8,128)(2,1)} async-done(((bf16[1,256,4,192]{1,3,0,2:T(8,128)(2,1)}), bf16[1,4096,4,192]{1,3,0,2:T(8,128)(2,1)}) %all-gather.11.cloned.1.call-update) | async-done | bytes 6291472 | tf_op jit(solution)/shard_map/all_gather | solution.py:57
  276.3 8.9 %fusion.115 = (f32[256,4]{0,1:T(4,128)S(1)}, bf16[256,4,1,192]{0,3,1,2:T(8,128)(2,1)}) fusion(bf16[256,4,192]{0,2,1:T(8,128)(2,1)} %convolution_convert_fusion.2, bf16[4,256,4096]{2,1,0:T(8,128)(2,1)} %copy-done.1, bf16[1,4096,4,192]{1,3,0,2:T(8,128)(2,1)} %all-gather.11.cloned.1.call-done), kind=kOutput, calls=%fused_computation.110 | convolution fusion | flops 1611398144 | bytes 15470592 | tf_op jit(solution)/shard_map/bhqk,kbhd->qbhd/dot_general | solution.py:68
  285.2 10.7 %multiply_convert_fusion = bf16[4,256,4096]{2,1,0:T(8,128)(2,1)S(1)} fusion(bf16[256,4,192]{0,2,1:T(8,128)(2,1)S(1)} %copy-done.10, f32[4,256]{1,0:T(4,128)S(1)} %bitcast.164, f32[4,256,4096]{2,1,0:T(8,128)} %get-tuple-element.25, f32[4,256]{1,0:T(4,128)S(1)} %get-tuple-element.24, bf16[1,4096,4,192]{1,3,0,2:T(8,128)(2,1)} %all-gather.11.cloned.1.call-done), kind=kOutput, calls=%fused_computation.1 | convolution fusion | flops 1627389952 | bytes 31858688 | tf_op jit(solution)/shard_map/qbhd,kbhd->bhqk/dot_general | solution.py:88
  295.9 3.5 copy-done.2
  299.4 4.6 fusion.14
  304.0 0.0 all-reduce.3.cloned.1.call-start
  304.1 0.9 copy-done.8
  305.0 3.5 fusion.23
  308.5 8.1 %fusion.95 = bf16[1,256,4,1,192]{1,4,2,3,0:T(8,128)(2,1)S(1)} fusion(bf16[4,256,4096]{2,1,0:T(8,128)(2,1)} %copy-done.2, bf16[1,4096,4,192]{1,3,0,2:T(8,128)(2,1)} %all-gather.13.cloned.1.call-done), kind=kOutput, calls=%fused_computation.83 | convolution fusion | flops 1611005952 | bytes 15073280 | tf_op jit(solution)/shard_map/bhqk,kbhd->qbhd/dot_general | solution.py:93
  316.6 50.1 %reduce-scatter.9.cloned.1.call-done = bf16[256,4,1,192]{0,3,1,2:T(8,128)(2,1)} async-done(((bf16[4096,4,1,192]{0,3,1,2:T(8,128)(2,1)}), bf16[256,4,1,192]{0,3,1,2:T(8,128)(2,1)}) %reduce-scatter.9.cloned.1.call-update) | async-done | bytes 393232 | tf_op jit(solution)/shard_map/reduce_scatter | solution.py:106
  366.8 92.3 %reduce-scatter.7.cloned.1.call-done = bf16[256,4,1,192]{0,3,1,2:T(8,128)(2,1)} async-done(((bf16[4096,4,1,192]{0,3,1,2:T(8,128)(2,1)}), bf16[256,4,1,192]{0,3,1,2:T(8,128)(2,1)}) %reduce-scatter.7.cloned.1.call-update) | async-done | bytes 393232 | tf_op jit(solution)/shard_map/reduce_scatter | solution.py:103
  459.1 5.3 fusion.18
  464.5 0.9 copy-done.12
  465.4 5.3 bitcast_convert_fusion
  470.7 0.3 reduce-scatter.5.cloned.1.call-start
  471.0 0.7 copy-done.7
  471.8 2.7 convolution_convert_fusion.1
  474.5 135.2 %all-reduce.3.cloned.1.call-done = (bf16[3,1536,192]{1,2,0:T(8,128)(2,1)}, bf16[192,1536]{1,0:T(8,128)(2,1)}) async-done(((bf16[3,1536,192]{1,2,0:T(8,128)(2,1)}, bf16[192,1536]{1,0:T(8,128)(2,1)}), (bf16[3,1536,192]{1,2,0:T(8,128)(2,1)}, bf16[192,1536]{1,0:T(8,128)(2,1)})) %all-reduce.3.cloned.1.call-update) | async-done | bytes 2359312 | tf_op jit(solution)/shard_map/psum | solution.py:142
  609.7 3.8 convert_element_type.130
  613.5 1.1 convert_element_type.132
  614.7 40.8 %reduce-scatter.11.cloned.1.call-done = bf16[32,4,1536]{2,0,1:T(8,128)(2,1)} async-done(((bf16[256,4,1536]{2,0,1:T(8,128)(2,1)}), bf16[32,4,1536]{2,0,1:T(8,128)(2,1)}) %reduce-scatter.11.cloned.1.call-update) | async-done | bytes 393232 | tf_op jit(solution)/shard_map/reduce_scatter | solution.py:117
  655.5 1.3 fusion.106
  656.8 46.8 %reduce-scatter.5.cloned.1.call-done = bf16[32,4,1536]{2,0,1:T(8,128)(2,1)} async-done(((bf16[256,4,1536]{2,0,1:T(8,128)(2,1)}), bf16[32,4,1536]{2,0,1:T(8,128)(2,1)}) %reduce-scatter.5.cloned.1.call-update) | async-done | bytes 393232 | tf_op jit(solution)/shard_map/reduce_scatter | solution.py:73
  703.5 2.2 fusion.110
  705.8 0.5 broadcast_in_dim.2
  706.3 2.2 mul.156
  708.6 2.9 fusion.60
  711.6 2.2 collective-permute-start.3
  713.8 2.5 fusion.31
  716.3 1.1 copy.18
  717.3 8.2 %collective-permute-start.2 = (bf16[2,4,1536]{2,0,1:T(2,128)(2,1)S(1)}, bf16[2,4,1536]{2,0,1:T(2,128)(2,1)S(1)}, u32[]{:S(2)}, u32[]{:S(2)}) collective-permute-start(bf16[2,4,1536]{2,0,1:T(2,128)(2,1)S(1)} %get-tuple-element.14), channel_id=1, source_target_pairs={{1,0},{2,1},{3,2},{4,3},{5,4},{6,5},{7,6},{8,7},{9,8},{10,9},{11,1... | collective-permute-start | bytes 73736 | tf_op jit(solution)/shard_map/ppermute | solution.py:18
  725.5 2.5 fusion.28
  728.0 2.5 fusion.24
  730.5 2.5 fusion.35
  733.0 2.6 fusion.89
  735.6 1.1 copy.19
  (44 shorter events, 0.5 us)
Async XLA Ops:
  7.2 77.1 %copy-start = (bf16[3,1536,192]{1,2,0:T(8,128)(2,1)S(1)}, bf16[3,1536,192]{1,2,0:T(8,128)(2,1)}, u32[]{:S(2)}) copy-start(bf16[3,1536,192]{1,2,0:T(8,128)(2,1)} %param.9) | copy-start | bytes 5308420
  7.2 77.1 %all-gather.7.cloned.1.call-start = ((), (), s32[]{:S(2)}) async-start(), calls=%async_computation.4 | async-start | bytes 3538944 | tf_op jit(solution)/shard_map/all_gather | solution.py:47
  8.4 11.7 %collective-permute-start.1 = (bf16[2,4,768]{2,0,1:T(2,128)(2,1)S(1)}, bf16[2,4,768]{2,0,1:T(2,128)(2,1)S(1)}, u32[]{:S(2)}, u32[]{:S(2)}) collective-permute-start(bf16[2,4,768]{2,0,1:T(2,128)(2,1)S(1)} %get-tuple-element.19), channel_id=1, source_target_pairs={{1,0},{2,1},{3,2},{4,3},{5,4},{6,5},{7,6},{8,7},{9,8},{10,9},{11,1... | collective-permute-start | bytes 36872 | tf_op jit(solution)/shard_map/ppermute | solution.py:18
  15.6 7.1 collective-permute-start
  34.2 4.3 copy-start.11
  37.2 2.4 copy-start.3
  39.5 90.9 %all-gather.9.cloned.1.call-start = ((), (), s32[]{:S(2)}) async-start(), calls=%async_computation.6 | async-start | bytes 3538944 | tf_op jit(solution)/shard_map/all_gather | solution.py:48
  40.4 165.2 %all-gather.13.cloned.1.call-start = ((), (), s32[]{:S(2)}) async-start(), calls=%async_computation.11 | async-start | bytes 6684672 | tf_op jit(solution)/shard_map/all_gather | solution.py:56
  89.2 187.1 %all-gather.11.cloned.1.call-start = ((), (), s32[]{:S(2)}) async-start(), calls=%async_computation.10 | async-start | bytes 6684672 | tf_op jit(solution)/shard_map/all_gather | solution.py:57
  89.8 277.0 %reduce-scatter.9.cloned.1.call-start = ((), (), s32[]{:S(2)}) async-start(), calls=%async_computation.8 | async-start | bytes 6684672 | tf_op jit(solution)/shard_map/reduce_scatter | solution.py:106
  234.9 10.8 %copy-start.9 = (bf16[256,4,192]{0,2,1:T(8,128)(2,1)S(1)}, bf16[256,4,192]{0,2,1:T(8,128)(2,1)}, u32[]{:S(2)}) copy-start(bf16[256,4,192]{0,2,1:T(8,128)(2,1)} %convolution_convert_fusion.2) | copy-start | bytes 1179652
  242.4 3.3 copy-start.1
  250.2 208.9 %reduce-scatter.7.cloned.1.call-start = ((), (), s32[]{:S(2)}) async-start(), calls=%async_computation.7 | async-start | bytes 6684672 | tf_op jit(solution)/shard_map/reduce_scatter | solution.py:103
  276.3 8.9 %copy-start.10 = (bf16[256,4,192]{0,2,1:T(8,128)(2,1)S(1)}, bf16[256,4,192]{0,2,1:T(8,128)(2,1)}, u32[]{:S(2)}) copy-start(bf16[256,4,192]{0,2,1:T(8,128)(2,1)} %convolution_convert_fusion.2) | copy-start | bytes 1179652
  295.9 3.5 copy-start.2
  304.0 1.0 copy-start.8
  304.0 305.7 %all-reduce.3.cloned.1.call-start = ((), (), s32[]{:S(2)}) async-start(), calls=%async_computation.12 | async-start | bytes 4718592 | tf_op jit(solution)/shard_map/psum | solution.py:142
  316.6 142.5 %copy-start.13 = (bf16[1,256,4,1,192]{1,4,2,3,0:T(8,128)(2,1)}, bf16[1,256,4,1,192]{1,4,2,3,0:T(8,128)(2,1)S(1)}, u32[]{:S(2)}) copy-start(bf16[1,256,4,1,192]{1,4,2,3,0:T(8,128)(2,1)S(1)} %fusion.95) | copy-start | bytes 1179652
  464.4 1.0 copy-start.12
  464.5 191.0 %reduce-scatter.11.cloned.1.call-start = ((), (), s32[]{:S(2)}) async-start(), calls=%async_computation.9 | async-start | bytes 3538944 | tf_op jit(solution)/shard_map/reduce_scatter | solution.py:117
  470.7 1.1 copy-start.7
  470.7 232.8 %reduce-scatter.5.cloned.1.call-start = ((), (), s32[]{:S(2)}) async-start(), calls=%async_computation.5 | async-start | bytes 3538944 | tf_op jit(solution)/shard_map/reduce_scatter | solution.py:73
  609.7 3.8 copy-start.6
  613.5 90.0 %copy-start.4 = (bf16[32,4,1536]{2,1,0:T(4,128)(2,1)S(1)}, bf16[32,4,1536]{2,1,0:T(4,128)(2,1)}, u32[]{:S(2)}) copy-start(bf16[32,4,1536]{2,1,0:T(4,128)(2,1)} %param.11) | copy-start | bytes 1179652
  711.6 4.7 copy-start.5
  711.6 13.9 %collective-permute-start.3 = (bf16[2,4,1536]{2,0,1:T(2,128)(2,1)S(1)}, bf16[2,4,1536]{2,0,1:T(2,128)(2,1)S(1)}, u32[]{:S(2)}, u32[]{:S(2)}) collective-permute-start(bf16[2,4,1536]{2,0,1:T(2,128)(2,1)S(1)} %get-tuple-element.15), channel_id=1, source_target_pairs={{0,1},{1,2},{2,3},{3,4},{4,5},{5,6},{6,7},{7,8},{8,9},{9,10},{10,1... | collective-permute-start | bytes 73736 | tf_op jit(solution)/shard_map/ppermute | solution.py:15
  717.3 13.2 %collective-permute-start.2 = (bf16[2,4,1536]{2,0,1:T(2,128)(2,1)S(1)}, bf16[2,4,1536]{2,0,1:T(2,128)(2,1)S(1)}, u32[]{:S(2)}, u32[]{:S(2)}) collective-permute-start(bf16[2,4,1536]{2,0,1:T(2,128)(2,1)S(1)} %get-tuple-element.14), channel_id=1, source_target_pairs={{1,0},{2,1},{3,2},{4,3},{5,4},{6,5},{7,6},{8,7},{9,8},{10,9},{11,1... | collective-permute-start | bytes 73736 | tf_op jit(solution)/shard_map/ppermute | solution.py:18
Sparse Core Ops, SparseCore 0:
  39.6 44.6 all-gather.6
  86.5 43.8 all-gather.8
  133.3 72.2 all-gather.12
  208.3 67.9 all-gather.10
  280.3 86.4 reduce-scatter.8
  370.8 88.2 reduce-scatter.6
  464.6 145.0 all-reduce.2
  612.1 43.3 reduce-scatter.10
  657.9 45.5 reduce-scatter.4
where the time goes:
time: 747 us; the launch traced here: 743 us
  waiting for transfers between devices  547 us (73%)
  matrix products  99.3 us (13%)
  other arithmetic  42.4 us (6%)
  starting transfers between devices  20.4 us (3%)
  local copies, waits for them, and re-layouts  19.4 us (3%)
  between operations  14.1 us (2%)
    psum x1, waiting for transfers between devices, body(): lax.psum(part_w_qkv.astype(jnp.bfloat16), 'seq').astype(jnp.float32)  135 us
    reduce_scatter x1, waiting for transfers between devices, body(): lax.psum_scatter(key_terms.astype(jnp.bfloat16), 'seq', scatter_dimension...  92.3 us
    all_gather x1, waiting for transfers between devices, body(): lax.all_gather(key_matrix, 'seq', axis=0, tiled=True)  71.3 us
    reduce_scatter x1, waiting for transfers between devices, body(): lax.psum_scatter(value_terms.astype(jnp.bfloat16), 'seq', scatter_dimensi...  50.1 us
    reduce_scatter x1, waiting for transfers between devices, body(): lax.psum_scatter(jnp.einsum('tbe,ec->tbc', piece, w_out, preferred_elemen...  46.8 us
    all_gather x1, waiting for transfers between devices, body(): normed_rows = lax.all_gather(normed, 'head', axis=0, tiled=True)  43.8 us
    reduce_scatter x1, waiting for transfers between devices, body(): lax.psum_scatter(jnp.einsum('itbe,ice->tbc', piece, w_qkv, preferred_elem...  40.8 us
    all_gather x1, waiting for transfers between devices, body(): grad_rows = lax.all_gather(grad_out, 'head', axis=0, tiled=True)  40.5 us
  transfers between devices with their start and end apart: 13, of which 10 were waited for; matrix products, arithmetic and copies ran while one was open for 15% of the time, Pallas kernels for 0%

commit v1 on v0

v1 whole, which is shorter than its diff:
```python
import math

import jax
import jax.numpy as jnp
from jax import lax
from jax.experimental import pallas as pl
from jax.experimental.pallas import tpu as pltpu
from jax.sharding import PartitionSpec as P

DH = 192
KW = 5
C = 1536
SCALE = DH ** (-0.5)
LOG2E = math.log2(math.e)
MESH = pl.DeviceIdType.MESH
F32 = jnp.float32
BF16 = jnp.bfloat16
VM = pltpu.VMEM


def coords():
    s = lax.axis_index("seq")
    h = lax.axis_index("head")
    return s // 4, (s // 2) % 2, s % 2, h // 4, h % 4


def device(y, zh, c, zl, x):
    return (y * 4 + zh * 2 + c, zl * 4 + x)


def x_peers():
    y, zh, c, zl, x = coords()
    return [device(y, zh, c, zl, (x + d) % 4) for d in (1, 2, 3)]


def zl_peer():
    y, zh, c, zl, x = coords()
    return device(y, zh, c, 1 - zl, x)


def core_peer():
    y, zh, c, zl, x = coords()
    return device(y, zh, 1 - c, zl, x)


def y_pair_peer():
    y, zh, c, zl, x = coords()
    return device(y + 1 - 2 * (y % 2), zh, c, zl, x)


def group():
    y, zh, c, zl, x = coords()
    return (y // 2) * 2 + zh


def group_peers():
    y, zh, c, zl, x = coords()
    peers = []
    for dy, dz in ((0, 1), (1, 0), (1, 1)):
        yh = (y // 2 + dy) % 2
        z2 = (zh + dz) % 2
        peers.append((yh * 2 + z2, device(yh * 2 + y % 2, z2, c, zl, x)))
    return peers


def barrier(peers):
    sem = pltpu.get_barrier_semaphore()
    for peer in peers:
        pl.semaphore_signal(sem, inc=1, device_id=peer, device_id_type=MESH)
    pl.semaphore_wait(sem, len(peers))


class Links:
    def __init__(self, send, recv):
        self.send, self.recv, self.used, self.all = send, recv, 0, []

    def start(self, src, dst, peer):
        copy = pltpu.make_async_remote_copy(
            src_ref=src,
            dst_ref=dst,
            send_sem=self.send.at[self.used],
            recv_sem=self.recv.at[self.used],
            device_id=peer,
            device_id_type=MESH,
        )
        self.used += 1
        self.all.append(copy)
        copy.start()
        return copy

    def finish(self):
        for copy in self.all:
            copy.wait_send()


def nt(a, b):
    return lax.dot_general(a, b, (((1,), (1,)), ((), ())), preferred_element_type=F32)


def nn(a, b):
    return lax.dot_general(a, b, (((1,), (0,)), ((), ())), preferred_element_type=F32)


class Gather:
    def __init__(self, links, buf):
        self.links, self.buf = links, buf
        y, zh, c, zl, x = coords()
        self.me = zl * 4 + x
        self.zl, self.x = zl, x

    def begin(self):
        own = self.buf.at[self.me]
        self.to_z = self.links.start(own, own, zl_peer())
        self.to_x = [self.links.start(own, own, peer) for peer in x_peers()]

    def forward(self):
        self.to_z.wait_recv()
        part = self.buf.at[(1 - self.zl) * 4 + self.x, pl.ds(0, 2)]
        self.fwd_x = [self.links.start(part, part, peer) for peer in x_peers()]
        self.fwd_z = []
        for d, copy in zip((1, 2, 3), self.to_x):
            copy.wait_recv()
            part = self.buf.at[self.zl * 4 + (self.x + 4 - d) % 4, pl.ds(2, 2)]
            self.fwd_z.append(self.links.start(part, part, zl_peer()))

    def end(self):
        for copy in self.fwd_x + self.fwd_z:
            copy.wait_recv()


def exchange_in(links, slab, buf, me):
    mine = group()
    buf[me, mine] = slab[mine]
    return [links.start(slab.at[g], buf.at[me, mine], peer) for g, peer in group_peers()]


class Scatter:
    def __init__(self, links, terms, first, second, last, pair, pair_sum, third, final):
        self.links, self.terms = links, terms
        self.first, self.second, self.last = first, second, last
        self.pair, self.pair_sum, self.third, self.final = pair, pair_sum, third, final
        y, zh, c, zl, x = coords()
        self.zl, self.x = zl, x
        self.me = zl * 4 + x

    def begin(self):
        zl, x, links = self.zl, self.x, self.links
        other = 1 - zl
        low, high = pl.ds(0, 64), pl.ds(64, 64)
        self.c_pair = [
            links.start(self.terms.at[other * 4 + k, high], self.pair.at[k], zl_peer()) for k in range(4)
        ]
        self.c_second = [
            links.start(self.terms.at[other * 4 + (x + d) % 4, low], self.second.at[d - 1], peer)
            for d, peer in zip((1, 2, 3), x_peers())
        ]
        self.c_first = [
            links.start(self.terms.at[zl * 4 + (x + d) % 4, low], self.first.at[d - 1], peer)
            for d, peer in zip((1, 2, 3), x_peers())
        ]

    def middle(self):
        zl, x, links = self.zl, self.x, self.links
        low, high = pl.ds(0, 64), pl.ds(64, 64)
        for copy in self.c_pair:
            copy.wait_recv()

        def add_pair(k, carry):
            self.pair_sum[k] = (
                self.terms[zl * 4 + k, high].astype(F32) + self.pair[k].astype(F32)
            ).astype(BF16)
            return carry

        lax.fori_loop(0, 4, add_pair, 0)
        self.c_third = [
            links.start(self.pair_sum.at[(x + d) % 4], self.third.at[d - 1], peer)
            for d, peer in zip((1, 2, 3), x_peers())
        ]
        for copy in self.c_second:
            copy.wait_recv()
        total = self.terms[(1 - zl) * 4 + x, low].astype(F32)
        for k in range(3):
            total = total + self.second[k].astype(F32)
        self.second[3] = total.astype(BF16)
        self.c_last = links.start(self.second.at[3], self.last, zl_peer())

    def end(self):
        zl, x = self.zl, self.x
        low = pl.ds(0, 64)
        for copy in self.c_first + self.c_third + [self.c_last]:
            copy.wait_recv()
        total = self.terms[self.me, low].astype(F32) + self.last[...].astype(F32)
        for k in range(3):
            total = total + self.first[k].astype(F32)
        self.final[0:2] = total.astype(BF16).reshape(2, 32, C)
        total = self.pair_sum[x].astype(F32)
        for k in range(3):
            total = total + self.third[k].astype(F32)
        self.final[2:4] = total.astype(BF16).reshape(2, 32, C)


SCATTER_SCRATCH = [
    VM((3, 64, C), BF16),
    VM((4, 64, C), BF16),
    VM((64, C), BF16),
    VM((4, 64, C), BF16),
    VM((4, 64, C), BF16),
    VM((3, 64, C), BF16),
    VM((4, 32, C), BF16),
]


def exchange_out(links, final, out):
    mine = group()
    out[mine] = final[mine]
    return [links.start(final.at[g], out.at[mine], peer) for g, peer in group_peers()]


def rows_of(ref, i):
    return ref[pl.ds(2 * i, 2)].reshape(256, C)


def gather_kernel(normed, grad, w, x_all, g_own, q, qt, kvt, send, recv):
    y, zh, c, zl, x = coords()
    me = zl * 4 + x
    barrier(x_peers() + [zl_peer()] + [peer for _, peer in group_peers()])
    links = Links(send, recv)
    copies = exchange_in(links, normed, x_all, me)
    for copy in copies:
        copy.wait_recv()
    gather = Gather(links, x_all)
    gather.begin()
    mine = group()
    g_own[mine] = grad[mine]
    copies = [links.start(grad.at[g], g_own.at[mine], peer) for g, peer in group_peers()]
    gather.forward()
    gather.end()

    def project(i, carry):
        rows = rows_of(x_all, i)
        part = nt(rows, w[0:DH])
        q[i] = part.astype(BF16)
        columns = pl.ds(pl.multiple_of(i * 256, 256), 256)
        qt[:, columns] = jnp.transpose(part).astype(BF16)
        kvt[:, columns] = nt(w[DH : 3 * DH], rows).astype(BF16)
        return carry

    lax.fori_loop(0, 4, project, 0)
    for copy in copies:
        copy.wait_recv()
    links.finish()


def attention_kernel(
    g_own, q, qt, kvt, w_out,
    mixed_out, gwo, dq_out, dqt_out, dkv_out,
    send, recv, g_all, kv, peak, chunk_peak, total, o_acc, e_all, ob, ot, do, dot_, delta,
    ds, dq_acc, acc, dkv_send, dkv_recv, terms, s1, s2, s3, s4, s5, s6, s7,
):
    y, zh, c, zl, x = coords()
    me = zl * 4 + x
    barrier(
        x_peers() + [zl_peer(), core_peer(), y_pair_peer()] + [peer for _, peer in group_peers()]
    )
    links = Links(send, recv)
    kv[0] = kvt[...]
    to_pair = links.start(kvt, kv.at[2], y_pair_peer())
    to_core = links.start(kvt, kv.at[1], core_peer())
    g_all[me] = g_own[...]
    gather = Gather(links, g_all)
    gather.begin()

    peak[...] = jnp.full_like(peak, -jnp.inf)
    total[...] = jnp.zeros_like(total)
    o_acc[...] = jnp.zeros_like(o_acc)
    unit = SCALE * LOG2E

    def forward(j):
        def tile(i, carry):
            s = nn(q[i], kv[j, 0:DH])
            old = peak[i]
            new = jnp.maximum(old, jnp.max(s, axis=-1, keepdims=True))
            peak[i] = new
            chunk_peak[j, i] = new
            fade = jnp.exp2((old - new) * unit)
            e = jnp.exp2(s * unit - new * unit)
            total[i] = total[i] * fade + jnp.sum(e, axis=-1, keepdims=True)
            eb = e.astype(BF16)
            e_all[j, i] = eb
            o_acc[i] = o_acc[i] * fade + nt(eb, kv[j, DH : 2 * DH])
            return carry

        lax.fori_loop(0, 4, tile, 0)

    forward(0)
    to_core.wait_recv()
    forward(1)
    to_pair.wait_recv()
    relay = links.start(kv.at[2], kv.at[3], core_peer())
    gather.forward()
    forward(2)
    relay.wait_recv()
    forward(3)

    def finish_tile(i, carry):
        inverse = 1.0 / total[i]
        o = o_acc[i] * inverse
        o_acc[i] = o
        ob[i] = o.astype(BF16)
        ot[:, pl.ds(pl.multiple_of(i * 256, 256), 256)] = jnp.transpose(o).astype(BF16)
        for j in range(4):
            chunk_peak[j, i] = jnp.exp2((chunk_peak[j, i] - peak[i]) * unit) * inverse
        term = nn(ob[i], w_out[...]).astype(BF16)
        terms[pl.ds(2 * i, 2)] = term.reshape(2, 128, C)
        return carry

    lax.fori_loop(0, 4, finish_tile, 0)
    scatter = Scatter(links, terms, s1, s2, s3, s4, s5, s6, s7)
    gather.end()
    scatter.begin()

    def output_gradient(i, carry):
        d = nt(rows_of(g_all, i), w_out[...])
        db = d.astype(BF16)
        do[i] = db
        db = db.astype(F32)
        dot_[:, pl.ds(pl.multiple_of(i * 256, 256), 256)] = jnp.transpose(db).astype(BF16)
        delta[i] = jnp.sum(db * o_acc[i], axis=-1, keepdims=True)
        dq_acc[i] = jnp.zeros((256, DH), F32)
        return carry

    lax.fori_loop(0, 4, output_gradient, 0)

    def backward(j):
        def tile(i, carry):
            p = e_all[j, i].astype(F32) * chunk_peak[j, i]
            e_all[j, i] = p.astype(BF16)
            dp = nn(do[i], kv[j, DH : 2 * DH])
            d = (p * (dp - delta[i])).astype(BF16)
            ds[i] = d
            dq_acc[i] += nt(d, kv[j, 0:DH])
            return carry

        lax.fori_loop(0, 4, tile, 0)

        def columns(n, carry):
            cut = pl.ds(pl.multiple_of(n * 256, 256), 256)
            acc[0:DH, cut] = nn(qt[...], ds[:, :, cut].reshape(1024, 256)) * SCALE
            acc[DH : 2 * DH, cut] = nn(dot_[...], e_all[j, :, :, cut].reshape(1024, 256))
            return carry

        lax.fori_loop(0, 4, columns, 0)

    backward(3)
    dkv_send[0] = acc[...].astype(BF16)
    far = links.start(dkv_send.at[0], dkv_recv.at[0], core_peer())
    backward(2)
    far.wait_recv()
    dkv_send[1] = (acc[...] + dkv_recv[0].astype(F32)).astype(BF16)
    pair = links.start(dkv_send.at[1], dkv_recv.at[1], y_pair_peer())
    backward(1)
    dkv_send[2] = acc[...].astype(BF16)
    near = links.start(dkv_send.at[2], dkv_recv.at[2], core_peer())
    scatter.middle()
    backward(0)

    def query(i, carry):
        d = dq_acc[i] * SCALE
        dq_out[i] = d.astype(BF16)
        dqt_out[:, pl.ds(pl.multiple_of(i * 256, 256), 256)] = jnp.transpose(d).astype(BF16)
        return carry

    lax.fori_loop(0, 4, query, 0)

    def w_out_gradient(n, carry):
        cut = pl.ds(pl.multiple_of(n * 512, 512), 512)
        gwo[:, cut] = nn(ot[...], g_all[:, :, :, cut].reshape(1024, 512)).astype(BF16)
        return carry

    lax.fori_loop(0, 3, w_out_gradient, 0)
    scatter.end()
    out = exchange_out(links, s7, mixed_out)
    near.wait_recv()
    pair.wait_recv()
    dkv_out[...] = (acc[...] + dkv_recv[1].astype(F32) + dkv_recv[2].astype(F32)).astype(BF16)
    for copy in out:
        copy.wait_recv()
    links.finish()


def chip_peers():
    y, zh, c, zl, x = coords()
    me = y * 2 + zh
    peers = []
    for d in range(1, 8):
        k = (me + d) % 8
        peers.append((k, device(k // 2, k % 2, c, zl, x)))
    return peers


def gradient_kernel(
    x_all, dq, dqt, dkv, w, gwo,
    normed_out, weights_out,
    send, recv, dkv_rows, terms, s1, s2, s3, s4, s5, s6, s7, part, half_in, half, piece_in, done,
):
    y, zh, c, zl, x = coords()
    me = zl * 4 + x
    chip = y * 2 + zh
    barrier(x_peers() + [zl_peer(), core_peer()] + [peer for _, peer in chip_peers()])
    links = Links(send, recv)

    def flip(i, carry):
        cut = pl.ds(pl.multiple_of(i * 256, 256), 256)
        dkv_rows[i] = jnp.transpose(dkv[:, cut].astype(F32)).astype(BF16)
        return carry

    lax.fori_loop(0, 4, flip, 0)

    def term(i, carry):
        t = nn(dq[i], w[0:DH]) + nn(dkv_rows[i], w[DH : 3 * DH])
        terms[pl.ds(2 * i, 2)] = t.astype(BF16).reshape(2, 128, C)
        return carry

    lax.fori_loop(0, 4, term, 0)
    scatter = Scatter(links, terms, s1, s2, s3, s4, s5, s6, s7)
    scatter.begin()

    def weights(n, carry):
        cut = pl.ds(pl.multiple_of(n * 512, 512), 512)
        rows = x_all[:, :, :, cut].reshape(1024, 512)
        part[0:4, :, cut] = nn(dqt[...], rows).astype(BF16).reshape(4, 48, 512)
        part[4:12, :, cut] = nn(dkv[...], rows).astype(BF16).reshape(8, 48, 512)
        part[12:16, :, cut] = gwo[:, cut].reshape(4, 48, 512)
        return carry

    lax.fori_loop(0, 3, weights, 0)
    swap = links.start(part.at[pl.ds((1 - c) * 8, 8)], half_in, core_peer())
    swap.wait_recv()

    def add_half(k, carry):
        half[k] = (part[c * 8 + k].astype(F32) + half_in[k].astype(F32)).astype(BF16)
        return carry

    lax.fori_loop(0, 8, add_half, 0)
    pieces = [
        links.start(half.at[k], piece_in.at[n], peer) for n, (k, peer) in enumerate(chip_peers())
    ]
    scatter.middle()
    for copy in pieces:
        copy.wait_recv()
    total = half[chip].astype(F32)
    for n in range(7):
        total = total + piece_in[n].astype(F32)
    done[c, chip] = total.astype(BF16)
    spread = [links.start(done.at[c, chip], done.at[c, chip], peer) for _, peer in chip_peers()]
    scatter.end()
    out = exchange_out(links, s7, normed_out)
    for copy in spread:
        copy.wait_recv()
    mirror = links.start(done.at[c], done.at[c], core_peer())
    mirror.wait_recv()

    def widen(k, carry):
        weights_out[k] = done[k // 8, k % 8].astype(F32)
        return carry

    lax.fori_loop(0, 16, widen, 0)
    for copy in out:
        copy.wait_recv()
    links.finish()


def vmem_call(kernel, collective_id, inputs, outputs, scratch, limit, copies):
    spec = pl.BlockSpec(memory_space=VM)
    return pl.pallas_call(
        kernel,
        out_shape=[jax.ShapeDtypeStruct(shape, dtype) for shape, dtype in outputs],
        in_specs=[spec] * len(inputs),
        out_specs=[spec] * len(outputs),
        scratch_shapes=[pltpu.SemaphoreType.DMA((copies,)), pltpu.SemaphoreType.DMA((copies,))] + scratch,
        compiler_params=pltpu.CompilerParams(
            collective_id=collective_id, has_side_effects=True, vmem_limit_bytes=limit << 20
        ),
    )(*inputs)


def shift_halo(low_rows, high_rows):
    forward = [(i, i + 1) for i in range(127)]
    backward = [(target, source) for source, target in forward]
    axes = ("seq", "head")
    return lax.ppermute(high_rows, axes, forward), lax.ppermute(low_rows, axes, backward)


def padded_2(block):
    low, high = shift_halo(block[:, :2], block[:, -2:])
    return jnp.concatenate([low, block, high], axis=1)


def body(enc_in, conv_weight, norm_gain, w_qkv, w_out, grad_out):
    enc = jnp.transpose(enc_in, (1, 0, 2))
    grad = jnp.transpose(grad_out, (1, 0, 2))
    w = jnp.transpose(w_qkv, (0, 2, 1)).reshape(3 * DH, C)
    padded = padded_2(enc)
    convolved = jnp.zeros((4, 64, C), F32)
    for offset in range(KW):
        convolved = convolved + jnp.einsum(
            "bti,io->bto", padded[:, offset : offset + 64], conv_weight[offset], preferred_element_type=F32
        )
    activated, gelu_pull = jax.vjp(jax.nn.gelu, convolved)
    skip = jnp.mean(activated.reshape(4, 32, 2, C), axis=2).astype(BF16)
    skip_wide = skip.astype(F32)
    inv_rms = lax.rsqrt(jnp.mean(skip_wide * skip_wide, axis=-1, keepdims=True) + 1e-06)
    normed = (skip_wide * inv_rms * norm_gain).astype(BF16)

    x_all, g_own, q, qt, kvt = vmem_call(
        gather_kernel,
        0,
        [normed, grad, w],
        [
            ((8, 4, 32, C), BF16),
            ((4, 32, C), BF16),
            ((4, 256, DH), BF16),
            ((DH, 1024), BF16),
            ((2 * DH, 1024), BF16),
        ],
        [],
        30,
        16,
    )
    head_sum, gwo, dq, dqt, dkv = vmem_call(
        attention_kernel,
        1,
        [g_own, q, qt, kvt, w_out],
        [
            ((4, 32, C), BF16),
            ((DH, C), BF16),
            ((4, 256, DH), BF16),
            ((DH, 1024), BF16),
            ((2 * DH, 1024), BF16),
        ],
        [
            VM((8, 4, 32, C), BF16),
            VM((4, 2 * DH, 1024), BF16),
            VM((4, 256, 1), F32),
            VM((4, 4, 256, 1), F32),
            VM((4, 256, 1), F32),
            VM((4, 256, DH), F32),
            VM((4, 4, 256, 1024), BF16),
            VM((4, 256, DH), BF16),
            VM((DH, 1024), BF16),
            VM((4, 256, DH), BF16),
            VM((DH, 1024), BF16),
            VM((4, 256, 1), F32),
            VM((4, 256, 1024), BF16),
            VM((4, 256, DH), F32),
            VM((2 * DH, 1024), F32),
            VM((3, 2 * DH, 1024), BF16),
            VM((3, 2 * DH, 1024), BF16),
            VM((8, 128, C), BF16),
        ]
        + SCATTER_SCRATCH,
        58,
        36,
    )
    d_normed, weights = vmem_call(
        gradient_kernel,
        2,
        [x_all, dq, dqt, dkv, w, gwo],
        [((4, 32, C), BF16), ((16, 48, C), F32)],
        [VM((4, 256, 2 * DH), BF16), VM((8, 128, C), BF16)]
        + SCATTER_SCRATCH
        + [
            VM((16, 48, C), BF16),
            VM((8, 48, C), BF16),
            VM((8, 48, C), BF16),
            VM((7, 48, C), BF16),
            VM((2, 8, 48, C), BF16),
        ],
        50,
        40,
    )
    mixed = (skip_wide + head_sum.astype(F32)).astype(BF16)
    d_normed = d_normed.astype(F32)
    unit_rows = skip_wide * inv_rms
    scaled = d_normed * norm_gain
    d_skip = grad.astype(F32) + inv_rms * (
        scaled - unit_rows * jnp.mean(scaled * unit_rows, axis=-1, keepdims=True)
    )
    d_act = jnp.repeat(d_skip, 2, axis=1) * 0.5
    d_conv = gelu_pull(d_act)[0].astype(BF16)
    d_pad = padded_2(d_conv)
    grad_input = jnp.zeros((4, 64, enc_in.shape[2]), F32)
    for offset in range(KW):
        grad_input = grad_input + jnp.einsum(
            "bto,io->bti",
            d_pad[:, 4 - offset : 4 - offset + 64],
            conv_weight[offset],
            preferred_element_type=F32,
        )
    weights = weights.reshape(4 * DH, C)
    return (
        jnp.transpose(mixed, (1, 0, 2)),
        jnp.transpose(grad_input.astype(BF16), (1, 0, 2)),
        jnp.transpose(weights[: 3 * DH].reshape(3, DH, C), (0, 2, 1)),
        weights[3 * DH :],
    )


def solution(mesh):
    return jax.shard_map(
        body,
        mesh=mesh,
        in_specs=(
            P(("seq", "head"), None, None),
            P(),
            P(),
            P(None, None, "head"),
            P("head", None),
            P(("seq", "head"), None, None),
        ),
        out_specs=(
            P(("seq", "head"), None, None),
            P(("seq", "head"), None, None),
            P(None, None, "head"),
            P("head", None),
        ),
        check_vma=False,
    )
```

time: 747 us -> 261 us (0.35)
  waiting for transfers between devices: 547 us -> 0.25 us
  Pallas kernels: 0 us -> 190 us
  matrix products: 99.3 us -> 21.5 us
  other arithmetic: 42.4 us -> 5.33 us
  between operations: 14.1 us -> 0.97 us
    reduce_scatter x4 -> x0, waiting for transfers between devices: 230 us -> none  [the longest x1 92.3 us: body(): lax.psum_scatter(key_terms.astype(jnp.bfloat16), 'seq', scatter_dimension...]
    pallas_call x0 -> x3, Pallas kernels: none -> 190 us  [vmem_call(): pl.pallas_call(kernel, out_shape=[jax.ShapeDtypeStruct(shape, dtype) for...]
    all_gather x4 -> x0, waiting for transfers between devices: 181 us -> none  [the longest x1 71.3 us: body(): lax.all_gather(key_matrix, 'seq', axis=0, tiled=True)]
    psum x1 -> x0, waiting for transfers between devices: 135 us -> none  [body(): lax.psum(part_w_qkv.astype(jnp.bfloat16), 'seq').astype(jnp.float32)]
    dot_general x22 -> x10, matrix products: 99.3 us -> 21.5 us  [the longest x5 13.8 us: body(): jnp.einsum('bti,io->bto', padded[:, offset:offset + 64], conv_weight[offs...]
    sub x1 -> x0, other arithmetic: 18.3 us -> none  [body(): exponent = jnp.exp(attention_logits - row_peak)]
    convert_element_type x5 -> x2, other arithmetic: 16.3 us -> 2.62 us  [the longest x1 2.45 us: body(): d_conv = gelu_pull(d_act)[0].astype(BF16)]
  transfers between devices with their start and end apart: 13 -> 4, of which waited for: 10 -> 1; matrix products, arithmetic and copies ran while one was open for 15% -> 7% of each run, Pallas kernels for 0% -> 0%
where the time goes in v1:
time: 261 us; the launch traced here: 257 us
  Pallas kernels  190 us (73%)
  local copies, waits for them, and re-layouts  22.7 us (9%)
  matrix products  21.5 us (8%)
  starting transfers between devices  16.8 us (6%)
  other arithmetic  5.33 us (2%)
    pallas_call x3, Pallas kernels, vmem_call(): pl.pallas_call(kernel, out_shape=[jax.ShapeDtypeStruct(shape, dtype) for...  190 us
    dot_general x5, matrix products, body(): jnp.einsum('bti,io->bto', padded[:, offset:offset + 64], conv_weight[offs...  13.8 us
    unnamed x38, local copies, waits for them, and re-layouts  13.4 us
    ppermute x2, starting transfers between devices, shift_halo(): lax.ppermute(low_rows, axes, backward)  11 us
    dot_general x5, matrix products, body(): jnp.einsum('bto,io->bti', d_pad[:, 4 - offset:4 - offset + 64], conv_weig...  7.66 us
    ppermute x2, starting transfers between devices, shift_halo(): lax.ppermute(high_rows, axes, forward)  5.87 us
  transfers between devices with their start and end apart: 4, of which 1 were waited for; matrix products, arithmetic and copies ran while one was open for 7% of the time, Pallas kernels for 0%

profile of v1, /device:TPU:1, one launch (start us, length us, event | category | flops | bytes accessed | tf_op | source)
XLA Modules:
  0.0 257.2 jit_solution(8438669983038393140)
XLA Ops:
  0.6 1.0 copy.20
  1.7 3.9 %collective-permute-start = (bf16[4,2,768]{2,1,0:T(2,128)(2,1)S(1)}, bf16[4,2,768]{2,1,0:T(2,128)(2,1)S(1)}, u32[]{:S(2)}, u32[]{:S(2)}) collective-permute-start(bf16[4,2,768]{2,1,0:T(2,128)(2,1)S(1)} %get-tuple-element.38), channel_id=1, source_target_pairs={{0,1},{1,2},{2,3},{3,4},{4,5},{5,6},{6,7},{7,8},{8,9},{9,10},{10,1... | collective-permute-start | bytes 36872 | tf_op jit(solution)/shard_map/ppermute | solution.py:491
  5.7 0.0 copy-start.10
  5.7 5.2 %collective-permute-start.1 = (bf16[4,2,768]{2,1,0:T(2,128)(2,1)S(1)}, bf16[4,2,768]{2,1,0:T(2,128)(2,1)S(1)}, u32[]{:S(2)}, u32[]{:S(2)}) collective-permute-start(bf16[4,2,768]{2,1,0:T(2,128)(2,1)S(1)} %get-tuple-element.39), channel_id=1, source_target_pairs={{1,0},{2,1},{3,2},{4,3},{5,4},{6,5},{7,6},{8,7},{9,8},{10,9},{11,1... | collective-permute-start | bytes 36872 | tf_op jit(solution)/shard_map/ppermute | solution.py:491
  10.9 2.6 %fusion.11 = f32[4,64,1536]{2,1,0:T(8,128)S(1)} fusion(bf16[5,768,1536]{2,1,0:T(8,128)(2,1)} %param.7, bf16[64,4,768]{2,1,0:T(4,128)(2,1)} %param.6), kind=kOutput, calls=%fused_computation.13 | convolution fusion | flops 603979776 | bytes 4325376 | tf_op jit(solution)/shard_map/bti,io->bto/dot_general | solution.py:506
  13.5 0.0 copy-done.10
  13.5 0.1 copy.19
  13.6 0.0 collective-permute-done.1
  13.6 2.4 fusion.4
  16.0 0.0 collective-permute-done
  16.0 2.4 fusion.15
  18.5 2.5 fusion.1
  21.0 3.9 %multiply_multiply_fusion.2 = (f32[4,64,1536]{2,1,0:T(8,128)S(1)}, f32[4,64,1536]{2,1,0:T(8,128)}) fusion(f32[4,64,1536]{2,1,0:T(8,128)S(1)} %fusion.4, f32[4,64,1536]{2,1,0:T(8,128)S(1)} %fusion.1, bf16[5,768,1536]{2,1,0:T(8,128)(2,1)} %param.7, bf16[4,64,768]{2,1,0:T(8,128)(2,1)S(1)} %bitcast.73, bf16[4,2,768]{2,1,0:T(2,128)(2,1)S(1)} %collective-permute-done.1), kind=kOutput, calls=%fused_computation.41 | convolution fusion | flops 608698368 | bytes 9056256 | tf_op jit(solution)/shard_map/bti,io->bto/dot_general | solution.py:506
  24.9 0.9 reshape.37
  25.8 0.0 copy-start.13
  25.8 1.9 reduce_sum.27
  27.7 0.0 copy-start
  27.7 0.2 fusion.68
  27.9 0.0 copy-done.13
  27.9 0.2 fusion.62.normed
  28.1 1.1 copy-done
  29.2 44.8 %shard_map.93 = (bf16[8,4,32,1536]{3,2,1,0:T(8,128)(2,1)S(1)}, bf16[4,32,1536]{2,1,0:T(8,128)(2,1)S(1)}, bf16[4,256,192]{2,1,0:T(8,128)(2,1)S(1)}, bf16[192,1024]{1,0:T(8,128)(2,1)S(1)}, bf16[384,1024]{1,0:T(8,128)(2,1)S(1)}) custom-call(bf16[4,32,1536]{2,1,0:T(8,128)(2,1)S(1)} %fusion.62.normed, bf16[4,32,1536]{2,1,0:T(8,128)(2,1)S(1)} %bitcast.67, ...), custom_call_target="tpu_custom_call" | custom-call | tf_op jit(solution)/shard_map/pallas_call | solution.py:475
  74.0 0.0 copy-start.1
  74.0 1.7 copy-done.1
  75.7 0.0 copy-start.3
  75.7 0.9 copy-done.3
  76.5 0.0 copy-start.6
  76.5 0.8 copy-done.6
  77.3 0.0 copy-start.8
  77.3 0.7 copy-done.8
  78.1 0.0 copy-start.9
  78.1 0.7 copy-done.9
  78.8 77.1 %shard_map.94 = (bf16[4,32,1536]{2,1,0:T(8,128)(2,1)}, bf16[192,1536]{1,0:T(8,128)(2,1)}, bf16[4,256,192]{2,1,0:T(8,128)(2,1)}, bf16[192,1024]{1,0:T(8,128)(2,1)}, bf16[384,1024]{1,0:T(8,128)(2,1)}) custom-call(bf16[4,32,1536]{2,1,0:T(8,128)(2,1)} %copy-done.8, bf16[4,256,192]{2,1,0:T(8,128)(2,1)} %copy-done.6, bf16[192,1024]{1,0:T(8,128)(2,1)} %copy-done.9, ...), custom_call_target="tpu_custom_call" | custom-call | tf_op jit(solution)/shard_map/pallas_call | solution.py:475
  156.0 0.0 copy-start.2
  156.0 1.1 copy-done.2
  157.1 1.1 copy-done.4
  158.2 1.0 copy-done.5
  159.2 1.0 copy-done.7
  160.2 67.6 %shard_map.95 = (bf16[4,32,1536]{2,1,0:T(8,128)(2,1)S(1)}, f32[16,48,1536]{2,1,0:T(8,128)}) custom-call(bf16[8,4,32,1536]{3,2,1,0:T(8,128)(2,1)} %copy-done.1, bf16[4,256,192]{2,1,0:T(8,128)(2,1)S(1)} %copy-done.5, bf16[192,1024]{1,0:T(8,128)(2,1)S(1)} %copy-done.7, bf16[384,1024]{1,0:T(8,128)(2,1)S(1)} %copy-done.2, bf16[576,1536]{1,0:T(8,128)(2,1)} %bitcast.65, ...), custom_call_target="tpu_custom_call" | custom-call | tf_op jit(solution)/shard_map/pallas_call | solution.py:475
  227.9 0.3 fusion.63
  228.1 0.0 copy-done.11
  228.1 0.0 copy-done.12
  228.1 0.4 fusion.67
  228.5 0.5 broadcast_in_dim.2
  229.1 1.1 mul.112
  230.2 2.5 fusion.36
  232.7 1.9 collective-permute-start.3
  234.6 0.0 slice-start
  234.6 2.6 %fusion.9 = f32[4,64,768]{2,1,0:T(8,128)S(1)} fusion(bf16[4,64,1536]{2,1,0:T(8,128)(2,1)S(1)} %fusion.36, bf16[5,768,1536]{2,1,0:T(8,128)(2,1)} %param.7), kind=kOutput, calls=%fused_computation.11 | convolution fusion | flops 603979776 | bytes 3932160 | tf_op jit(solution)/shard_map/bto,io->bti/dot_general | solution.py:594
  237.3 0.0 slice-start.1
  237.3 2.5 slice.92
  239.8 4.2 %slice.91 = f32[12,48,1536]{2,1,0:T(8,128)} slice(f32[16,48,1536]{2,1,0:T(8,128)} %get-tuple-element.27), slice={[0:12], [0:48], [0:1536]} | slice | bytes 7077888 | tf_op jit(solution)/shard_map/slice | solution.py:604
  244.0 1.1 copy.12
  245.0 5.7 %collective-permute-start.2 = (bf16[4,2,1536]{2,1,0:T(2,128)(2,1)S(1)}, bf16[4,2,1536]{2,1,0:T(2,128)(2,1)S(1)}, u32[]{:S(2)}, u32[]{:S(2)}) collective-permute-start(bf16[4,2,1536]{2,1,0:T(2,128)(2,1)S(1)} %get-tuple-element.34), channel_id=1, source_target_pairs={{1,0},{2,1},{3,2},{4,3},{5,4},{6,5},{7,6},{8,7},{9,8},{10,9},{11,1... | collective-permute-start | bytes 73736 | tf_op jit(solution)/shard_map/ppermute | solution.py:491
  250.8 0.0 collective-permute-done.3
  250.8 2.5 fusion.6
  253.3 0.0 slice-done
  253.3 0.0 slice-done.1
  253.3 0.0 slice-done.2
  253.3 0.8 fusion.2
  254.2 0.2 collective-permute-done.2
  254.4 0.8 fusion.13
  255.2 0.9 fusion.52
  256.1 1.1 copy.13
  (11 shorter events, 0.1 us)
Async XLA Ops:
  1.7 14.3 %collective-permute-start = (bf16[4,2,768]{2,1,0:T(2,128)(2,1)S(1)}, bf16[4,2,768]{2,1,0:T(2,128)(2,1)S(1)}, u32[]{:S(2)}, u32[]{:S(2)}) collective-permute-start(bf16[4,2,768]{2,1,0:T(2,128)(2,1)S(1)} %get-tuple-element.38), channel_id=1, source_target_pairs={{0,1},{1,2},{2,3},{3,4},{4,5},{5,6},{6,7},{7,8},{8,9},{9,10},{10,1... | collective-permute-start | bytes 36872 | tf_op jit(solution)/shard_map/ppermute | solution.py:491
  5.7 7.8 %copy-start.10 = (bf16[32,4,1536]{2,1,0:T(4,128)(2,1)S(1)}, bf16[32,4,1536]{2,1,0:T(4,128)(2,1)}, u32[]{:S(2)}) copy-start(bf16[32,4,1536]{2,1,0:T(4,128)(2,1)} %param.11) | copy-start | bytes 1179652
  5.7 7.9 %collective-permute-start.1 = (bf16[4,2,768]{2,1,0:T(2,128)(2,1)S(1)}, bf16[4,2,768]{2,1,0:T(2,128)(2,1)S(1)}, u32[]{:S(2)}, u32[]{:S(2)}) collective-permute-start(bf16[4,2,768]{2,1,0:T(2,128)(2,1)S(1)} %get-tuple-element.39), channel_id=1, source_target_pairs={{1,0},{2,1},{3,2},{4,3},{5,4},{6,5},{7,6},{8,7},{9,8},{10,9},{11,1... | collective-permute-start | bytes 36872 | tf_op jit(solution)/shard_map/ppermute | solution.py:491
  25.8 2.1 copy-start.13
  27.7 1.5 copy-start
  74.0 1.7 copy-start.1
  75.7 0.9 copy-start.3
  76.5 0.8 copy-start.6
  77.3 0.7 copy-start.8
  78.1 0.7 copy-start.9
  156.0 1.1 copy-start.2
  157.1 1.1 copy-start.4
  158.2 1.0 copy-start.5
  159.2 1.0 copy-start.7
  160.2 67.9 %copy-start.11 = (bf16[32,4,1536]{2,1,0:T(4,128)(2,1)S(1)}, bf16[32,4,1536]{2,1,0:T(4,128)(2,1)}, u32[]{:S(2)}) copy-start(bf16[32,4,1536]{2,1,0:T(4,128)(2,1)} %param.11) | copy-start | bytes 1179652
  160.2 67.9 %copy-start.12 = (bf16[4,32,1536]{2,1,0:T(8,128)(2,1)S(1)}, bf16[4,32,1536]{2,1,0:T(8,128)(2,1)}, u32[]{:S(2)}) copy-start(bf16[4,32,1536]{2,1,0:T(8,128)(2,1)} %get-tuple-element.20) | copy-start | bytes 1179652
  232.7 18.1 %collective-permute-start.3 = (bf16[4,2,1536]{2,1,0:T(2,128)(2,1)S(1)}, bf16[4,2,1536]{2,1,0:T(2,128)(2,1)S(1)}, u32[]{:S(2)}, u32[]{:S(2)}) collective-permute-start(bf16[4,2,1536]{2,1,0:T(2,128)(2,1)S(1)} %get-tuple-element.35), channel_id=1, source_target_pairs={{0,1},{1,2},{2,3},{3,4},{4,5},{5,6},{6,7},{7,8},{8,9},{9,10},{10,1... | collective-permute-start | bytes 73736 | tf_op jit(solution)/shard_map/ppermute | solution.py:491
  234.6 18.7 %slice-start = ((s8[11796480]{0:T(1024)(128)(4,1)}), s8[4194304]{0:T(1024)(128)(4,1)S(1)}, s32[]{:S(2)}) async-start(s8[11796480]{0:T(1024)(128)(4,1)} %bitcast.75), calls=%async_computation | async-start | bytes 8388608
  237.3 16.0 %slice-start.1 = ((s8[11796480]{0:T(1024)(128)(4,1)}), s8[4194304]{0:T(1024)(128)(4,1)S(1)}, s32[]{:S(2)}) async-start(s8[11796480]{0:T(1024)(128)(4,1)} %bitcast.75), calls=%async_computation.1 | async-start | bytes 8388608
  239.8 13.5 %slice-start.2 = ((s8[11796480]{0:T(1024)(128)(4,1)}), s8[3407872]{0:T(1024)(128)(4,1)S(1)}, s32[]{:S(2)}) async-start(s8[11796480]{0:T(1024)(128)(4,1)} %bitcast.75), calls=%async_computation.2 | async-start | bytes 6815744
  245.0 9.4 %collective-permute-start.2 = (bf16[4,2,1536]{2,1,0:T(2,128)(2,1)S(1)}, bf16[4,2,1536]{2,1,0:T(2,128)(2,1)S(1)}, u32[]{:S(2)}, u32[]{:S(2)}) collective-permute-start(bf16[4,2,1536]{2,1,0:T(2,128)(2,1)S(1)} %get-tuple-element.34), channel_id=1, source_target_pairs={{1,0},{2,1},{3,2},{4,3},{5,4},{6,5},{7,6},{8,7},{9,8},{10,9},{11,1... | collective-permute-start | bytes 73736 | tf_op jit(solution)/shard_map/ppermute | solution.py:491

commit v2 on v1

--- a/solution.py
+++ b/solution.py
@@ -63,11 +63,15 @@
     return peers
 
 
-def barrier(peers):
+def greet(peers):
     sem = pltpu.get_barrier_semaphore()
     for peer in peers:
         pl.semaphore_signal(sem, inc=1, device_id=peer, device_id_type=MESH)
-    pl.semaphore_wait(sem, len(peers))
+    return len(peers)
+
+
+def met(count):
+    pl.semaphore_wait(pltpu.get_barrier_semaphore(), count)
 
 
 class Links:
@@ -101,30 +105,80 @@
     return lax.dot_general(a, b, (((1,), (0,)), ((), ())), preferred_element_type=F32)
 
 
+def x_neighbours():
+    y, zh, c, zl, x = coords()
+    return device(y, zh, c, zl, (x + 1) % 4), device(y, zh, c, zl, (x + 3) % 4)
+
+
 class Gather:
     def __init__(self, links, buf):
         self.links, self.buf = links, buf
         y, zh, c, zl, x = coords()
-        self.me = zl * 4 + x
         self.zl, self.x = zl, x
-
-    def begin(self):
-        own = self.buf.at[self.me]
-        self.to_z = self.links.start(own, own, zl_peer())
-        self.to_x = [self.links.start(own, own, peer) for peer in x_peers()]
+        self.order = [group()] + [g for g, _ in group_peers()]
+
+    def at(self, plane, dx, r):
+        return self.buf.at[plane * 4 + (self.x + dx) % 4, self.order[r]]
+
+    def begin(self, incoming):
+        up, down = x_neighbours()
+        start = self.links.start
+        self.up, self.down, self.z = {}, {}, {}
+        for r in range(4):
+            if r > 0 and incoming is not None:
+                incoming[r - 1].wait_recv()
+            own = self.at(self.zl, 0, r)
+            self.up[r] = start(own, own, up)
+            self.down[r] = start(own, own, down)
+            self.z[r] = start(own, own, zl_peer())
 
     def forward(self):
-        self.to_z.wait_recv()
-        part = self.buf.at[(1 - self.zl) * 4 + self.x, pl.ds(0, 2)]
-        self.fwd_x = [self.links.start(part, part, peer) for peer in x_peers()]
-        self.fwd_z = []
-        for d, copy in zip((1, 2, 3), self.to_x):
-            copy.wait_recv()
-            part = self.buf.at[self.zl * 4 + (self.x + 4 - d) % 4, pl.ds(2, 2)]
-            self.fwd_z.append(self.links.start(part, part, zl_peer()))
+        up, down = x_neighbours()
+        z, zl, other = zl_peer(), self.zl, 1 - self.zl
+        self.rest = []
+
+        def send(part, peer):
+            return self.links.start(part, part, peer)
+
+        self.up[0].wait_recv()
+        self.relay_0 = send(self.at(zl, 3, 0), up)
+        self.rest.append(send(self.at(zl, 3, 0), z))
+        self.down[1].wait_recv()
+        self.relay_1 = send(self.at(zl, 1, 1), down)
+        self.rest.append(send(self.at(zl, 1, 1), z))
+        self.z[2].wait_recv()
+        self.over_2 = send(self.at(other, 0, 2), up)
+        self.rest.append(send(self.at(other, 0, 2), down))
+        self.z[3].wait_recv()
+        self.over_3 = send(self.at(other, 0, 3), down)
+        self.rest.append(send(self.at(other, 0, 3), up))
+        self.down[0].wait_recv()
+        self.rest.append(send(self.at(zl, 1, 0), z))
+        self.up[1].wait_recv()
+        self.rest.append(send(self.at(zl, 3, 1), z))
+        self.up[2].wait_recv()
+        self.rest.append(send(self.at(zl, 3, 2), up))
+        self.down[3].wait_recv()
+        self.rest.append(send(self.at(zl, 1, 3), down))
+
+    def relay(self):
+        up, down = x_neighbours()
+        z, zl, other = zl_peer(), self.zl, 1 - self.zl
+
+        def send(part, peer):
+            self.rest.append(self.links.start(part, part, peer))
+
+        self.relay_0.wait_recv()
+        send(self.at(zl, 2, 0), z)
+        self.relay_1.wait_recv()
+        send(self.at(zl, 2, 1), z)
+        self.over_2.wait_recv()
+        send(self.at(other, 3, 2), up)
+        self.over_3.wait_recv()
+        send(self.at(other, 1, 3), down)
 
     def end(self):
-        for copy in self.fwd_x + self.fwd_z:
+        for copy in self.rest + [self.up[3], self.down[2], self.z[0], self.z[1]]:
             copy.wait_recv()
 
 
@@ -143,7 +197,7 @@
         self.zl, self.x = zl, x
         self.me = zl * 4 + x
 
-    def begin(self):
+    def begin_other(self):
         zl, x, links = self.zl, self.x, self.links
         other = 1 - zl
         low, high = pl.ds(0, 64), pl.ds(64, 64)
@@ -154,6 +208,10 @@
             links.start(self.terms.at[other * 4 + (x + d) % 4, low], self.second.at[d - 1], peer)
             for d, peer in zip((1, 2, 3), x_peers())
         ]
+
+    def begin_own(self):
+        zl, x, links = self.zl, self.x, self.links
+        low = pl.ds(0, 64)
         self.c_first = [
             links.start(self.terms.at[zl * 4 + (x + d) % 4, low], self.first.at[d - 1], peer)
             for d, peer in zip((1, 2, 3), x_peers())
@@ -220,20 +278,89 @@
     return ref[pl.ds(2 * i, 2)].reshape(256, C)
 
 
-def gather_kernel(normed, grad, w, x_all, g_own, q, qt, kvt, send, recv):
+def slab_peers():
+    me = lax.axis_index("seq") * 8 + lax.axis_index("head")
+    after, before = (me + 1) % 128, (me + 127) % 128
+    return (after // 8, after % 8), (before // 8, before % 8)
+
+
+def shifted(block, edge, up, here):
+    width = block.shape[-1]
+    wide = block.astype(F32)
+    place = lax.broadcasted_iota(jnp.int32, (128, width), 0) % 32
+    fill = jnp.where(here, edge.astype(F32), 0.0)
+    fill = jnp.concatenate([jnp.broadcast_to(fill[b : b + 1], (32, width)) for b in range(4)], axis=0)
+    if up:
+        return jnp.where(place == 31, fill, pltpu.roll(wide, 127, 0)).astype(BF16)
+    return jnp.where(place == 0, fill, pltpu.roll(wide, 1, 0)).astype(BF16)
+
+
+def gather_kernel(
+    enc, edges, gain, grad, w, conv_w,
+    skip, rstd, slope, x_all, g_own, q, qt, kvt,
+    send, recv, w_sem, w_buf, halo, taps, normed,
+):
     y, zh, c, zl, x = coords()
     me = zl * 4 + x
-    barrier(x_peers() + [zl_peer()] + [peer for _, peer in group_peers()])
+    slab = lax.axis_index("seq") * 8 + lax.axis_index("head")
+    after, before = slab_peers()
+
+    def tile_copy(n):
+        cut = pl.ds(pl.multiple_of(n * 256, 256), 256)
+        return pltpu.make_async_copy(conv_w.at[:, :, cut], w_buf.at[n], w_sem.at[n])
+
+    for n in range(6):
+        tile_copy(n).start()
+    met(greet([*x_neighbours(), zl_peer(), after, before] + [peer for _, peer in group_peers()]))
     links = Links(send, recv)
+    to_after = links.start(edges.at[1], halo.at[0], after)
+    to_before = links.start(edges.at[0], halo.at[1], before)
+    mine = group()
+    even, odd = enc[0].reshape(128, 768), enc[1].reshape(128, 768)
+    low, high = pl.ds(0, 128), pl.ds(128, 128)
+    taps[2, low], taps[2, high] = even, odd
+    taps[3, low], taps[1, high] = odd, even
+    to_after.wait_recv()
+    to_before.wait_recv()
+    first, last = slab > 0, slab < 127
+    even_before = shifted(even, halo[0, 0], False, first)
+    odd_before = shifted(odd, halo[0, 1], False, first)
+    even_after = shifted(even, halo[1, 0], True, last)
+    odd_after = shifted(odd, halo[1, 1], True, last)
+    taps[0, low], taps[0, high] = even_before, odd_before
+    taps[1, low], taps[3, high] = odd_before, even_after
+    taps[4, low], taps[4, high] = even_after, odd_after
+    root = math.sqrt(2.0 / math.pi)
+
+    def conv_tile(n, squares):
+        tile_copy(n).wait()
+        cut = pl.ds(pl.multiple_of(n * 256, 256), 256)
+        v = nn(taps[0], w_buf[n, 0])
+        for k in range(1, KW):
+            v = v + nn(taps[k], w_buf[n, k])
+        v2 = v * v
+        t = jnp.tanh(root * v * (1.0 + 0.044715 * v2))
+        half = 0.5 * (1.0 + t)
+        act = v * half
+        pull = half + 0.5 * v * (1.0 - t * t) * (root * (1.0 + 3.0 * 0.044715 * v2))
+        slope[:, cut] = pull * 0.5
+        s = ((act[0:128] + act[128:256]) * 0.5).astype(BF16)
+        skip[:, :, cut] = s.reshape(4, 32, 256)
+        s = s.astype(F32)
+        return squares + jnp.sum(s * s, axis=-1, keepdims=True)
+
+    squares = lax.fori_loop(0, 6, conv_tile, jnp.zeros((128, 1), F32))
+    r = lax.rsqrt(squares / C + 1e-06)
+    rstd[...] = r
+    value = skip[...].reshape(128, C).astype(F32) * r * gain[...]
+    normed[...] = value.astype(BF16).reshape(4, 32, C)
     copies = exchange_in(links, normed, x_all, me)
-    for copy in copies:
-        copy.wait_recv()
     gather = Gather(links, x_all)
-    gather.begin()
-    mine = group()
+    gather.begin(copies)
     g_own[mine] = grad[mine]
     copies = [links.start(grad.at[g], g_own.at[mine], peer) for g, peer in group_peers()]
     gather.forward()
+    gather.relay()
     gather.end()
 
     def project(i, carry):
@@ -255,20 +382,18 @@
     g_own, q, qt, kvt, w_out,
     mixed_out, gwo, dq_out, dqt_out, dkv_out,
     send, recv, g_all, kv, peak, chunk_peak, total, o_acc, e_all, ob, ot, do, dot_, delta,
-    ds, dq_acc, acc, dkv_send, dkv_recv, terms, s1, s2, s3, s4, s5, s6, s7,
+    ds, dq_acc, acc, dkv_send, dkv_recv, terms, s1, s2, s3, s4, s5, s6,
 ):
     y, zh, c, zl, x = coords()
     me = zl * 4 + x
-    barrier(
-        x_peers() + [zl_peer(), core_peer(), y_pair_peer()] + [peer for _, peer in group_peers()]
-    )
+    met(greet(x_peers() + [zl_peer(), core_peer(), y_pair_peer()]))
     links = Links(send, recv)
     kv[0] = kvt[...]
     to_pair = links.start(kvt, kv.at[2], y_pair_peer())
     to_core = links.start(kvt, kv.at[1], core_peer())
     g_all[me] = g_own[...]
     gather = Gather(links, g_all)
-    gather.begin()
+    gather.begin(None)
 
     peak[...] = jnp.full_like(peak, -jnp.inf)
     total[...] = jnp.zeros_like(total)
@@ -290,14 +415,15 @@
             o_acc[i] = o_acc[i] * fade + nt(eb, kv[j, DH : 2 * DH])
             return carry
 
-        lax.fori_loop(0, 4, tile, 0)
+        lax.fori_loop(0, 4, tile, 0, unroll=True)
 
     forward(0)
     to_core.wait_recv()
     forward(1)
+    gather.forward()
     to_pair.wait_recv()
     relay = links.start(kv.at[2], kv.at[3], core_peer())
-    gather.forward()
+    gather.relay()
     forward(2)
     relay.wait_recv()
     forward(3)
@@ -315,9 +441,10 @@
         return carry
 
     lax.fori_loop(0, 4, finish_tile, 0)
-    scatter = Scatter(links, terms, s1, s2, s3, s4, s5, s6, s7)
+    scatter = Scatter(links, terms, s1, s2, s3, s4, s5, s6, mixed_out)
     gather.end()
-    scatter.begin()
+    scatter.begin_other()
+    scatter.begin_own()
 
     def output_gradient(i, carry):
         d = nt(rows_of(g_all, i), w_out[...])
@@ -341,7 +468,7 @@
             dq_acc[i] += nt(d, kv[j, 0:DH])
             return carry
 
-        lax.fori_loop(0, 4, tile, 0)
+        lax.fori_loop(0, 4, tile, 0, unroll=True)
 
         def columns(n, carry):
             cut = pl.ds(pl.multiple_of(n * 256, 256), 256)
@@ -379,103 +506,207 @@
 
     lax.fori_loop(0, 3, w_out_gradient, 0)
     scatter.end()
-    out = exchange_out(links, s7, mixed_out)
     near.wait_recv()
     pair.wait_recv()
     dkv_out[...] = (acc[...] + dkv_recv[1].astype(F32) + dkv_recv[2].astype(F32)).astype(BF16)
-    for copy in out:
-        copy.wait_recv()
     links.finish()
 
 
-def chip_peers():
-    y, zh, c, zl, x = coords()
-    me = y * 2 + zh
-    peers = []
-    for d in range(1, 8):
-        k = (me + d) % 8
-        peers.append((k, device(k // 2, k % 2, c, zl, x)))
-    return peers
+def y_peers():
+    y, zh, c, zl, x = coords()
+    return [((y + d) % 4, device((y + d) % 4, zh, c, zl, x)) for d in (1, 2, 3)]
+
+
+def zh_peer():
+    y, zh, c, zl, x = coords()
+    return device(y, 1 - zh, c, zl, x)
+
+
+class Sum:
+    def __init__(self, links, part, half_in, half, y_in, z_in, done):
+        self.links, self.part, self.half_in, self.half = links, part, half_in, half
+        self.y_in, self.z_in, self.done = y_in, z_in, done
+        self.y, zh, self.c, zl, x = coords()
+
+    def swap(self):
+        self.c_swap = self.links.start(self.part.at[1 - self.c], self.half_in, core_peer())
+
+    def over_y(self):
+        self.c_swap.wait_recv()
+
+        def add(k, carry):
+            self.half[k] = (self.part[self.c, k].astype(F32) + self.half_in[k].astype(F32)).astype(BF16)
+            return carry
+
+        lax.fori_loop(0, 4, add, 0)
+        self.c_y = [
+            self.links.start(self.half.at[k], self.y_in.at[n], peer) for n, (k, peer) in enumerate(y_peers())
+        ]
+
+    def over_z(self):
+        for copy in self.c_y:
+            copy.wait_recv()
+        total = self.half[self.y].astype(F32)
+        for n in range(3):
+            total = total + self.y_in[n].astype(F32)
+        self.z_in[0] = total.astype(BF16)
+        self.c_z = self.links.start(self.z_in.at[0], self.z_in.at[1], zh_peer())
+
+    def spread(self):
+        self.c_z.wait_recv()
+        total = self.z_in[0].astype(F32) + self.z_in[1].astype(F32)
+        self.done[self.c, self.y] = total.astype(BF16)
+        piece = self.done.at[self.c, self.y]
+        self.c_spread = [self.links.start(piece, piece, peer) for _, peer in y_peers()]
+
+    def mirror(self):
+        for copy in self.c_spread:
+            copy.wait_recv()
+        rows = self.done.at[self.c]
+        self.c_mirror = self.links.start(rows, rows, core_peer())
+
+    def end(self):
+        self.c_mirror.wait_recv()
+
+
+SUM_SCRATCH = [
+    VM((2, 4, 48, C), BF16),
+    VM((4, 48, C), BF16),
+    VM((4, 48, C), BF16),
+    VM((3, 48, C), BF16),
+    VM((2, 48, C), BF16),
+    VM((2, 4, 48, C), BF16),
+]
 
 
 def gradient_kernel(
-    x_all, dq, dqt, dkv, w, gwo,
-    normed_out, weights_out,
-    send, recv, dkv_rows, terms, s1, s2, s3, s4, s5, s6, s7, part, half_in, half, piece_in, done,
+    x_all, dq, dqt, dkv, w, gwo, mixed_in, skip, rstd, gain, slope, grad, conv_w,
+    mixed_out, gw_out, gwo_out, grad_input,
+    send, recv, w_sem, dkv_rows, terms, s1, s2, s3, s4, s5, s6, s7,
+    a1, a2, a3, a4, a5, a6, b1, b2, b3, b4, b5, b6, w_buf, d_normed, edges, halo, taps,
 ):
     y, zh, c, zl, x = coords()
-    me = zl * 4 + x
-    chip = y * 2 + zh
-    barrier(x_peers() + [zl_peer(), core_peer()] + [peer for _, peer in chip_peers()])
-    links = Links(send, recv)
+    slab = lax.axis_index("seq") * 8 + lax.axis_index("head")
+    after, before = slab_peers()
+    w_copy = pltpu.make_async_copy(conv_w, w_buf, w_sem)
+    w_copy.start()
+    count = greet(
+        x_peers()
+        + [zl_peer(), core_peer(), zh_peer(), after, before]
+        + [peer for _, peer in y_peers()]
+        + [peer for _, peer in group_peers()]
+    )
 
     def flip(i, carry):
         cut = pl.ds(pl.multiple_of(i * 256, 256), 256)
         dkv_rows[i] = jnp.transpose(dkv[:, cut].astype(F32)).astype(BF16)
         return carry
 
-    lax.fori_loop(0, 4, flip, 0)
-
-    def term(i, carry):
-        t = nn(dq[i], w[0:DH]) + nn(dkv_rows[i], w[DH : 3 * DH])
-        terms[pl.ds(2 * i, 2)] = t.astype(BF16).reshape(2, 128, C)
+    lax.fori_loop(0, 4, flip, 0, unroll=True)
+
+    def query_weights(n, carry):
+        cut = pl.ds(pl.multiple_of(n * 512, 512), 512)
+        rows = x_all[:, :, :, cut].reshape(1024, 512)
+        a1[0, :, :, cut] = nn(dqt[...], rows).astype(BF16).reshape(4, 48, 512)
+        a1[1, :, :, cut] = gwo[:, cut].reshape(4, 48, 512)
         return carry
 
-    lax.fori_loop(0, 4, term, 0)
+    lax.fori_loop(0, 3, query_weights, 0)
+    met(count)
+    links = Links(send, recv)
+    early = Sum(links, a1, a2, a3, a4, a5, a6)
+    late = Sum(links, b1, b2, b3, b4, b5, b6)
+    early.swap()
+
+    def terms_of(plane):
+        def term(k, carry):
+            i = plane * 2 + k
+            t = nn(dq[i], w[0:DH]) + nn(dkv_rows[i], w[DH : 3 * DH])
+            terms[pl.ds(2 * i, 2)] = t.astype(BF16).reshape(2, 128, C)
+            return carry
+
+        lax.fori_loop(0, 2, term, 0)
+
     scatter = Scatter(links, terms, s1, s2, s3, s4, s5, s6, s7)
-    scatter.begin()
+    terms_of(1 - zl)
+    scatter.begin_other()
+    terms_of(zl)
+    scatter.begin_own()
+    early.over_y()
 
     def weights(n, carry):
         cut = pl.ds(pl.multiple_of(n * 512, 512), 512)
         rows = x_all[:, :, :, cut].reshape(1024, 512)
-        part[0:4, :, cut] = nn(dqt[...], rows).astype(BF16).reshape(4, 48, 512)
-        part[4:12, :, cut] = nn(dkv[...], rows).astype(BF16).reshape(8, 48, 512)
-        part[12:16, :, cut] = gwo[:, cut].reshape(4, 48, 512)
+        b1[:, :, :, cut] = nn(dkv[...], rows).astype(BF16).reshape(2, 4, 48, 512)
         return carry
 
     lax.fori_loop(0, 3, weights, 0)
-    swap = links.start(part.at[pl.ds((1 - c) * 8, 8)], half_in, core_peer())
-    swap.wait_recv()
-
-    def add_half(k, carry):
-        half[k] = (part[c * 8 + k].astype(F32) + half_in[k].astype(F32)).astype(BF16)
-        return carry
-
-    lax.fori_loop(0, 8, add_half, 0)
-    pieces = [
-        links.start(half.at[k], piece_in.at[n], peer) for n, (k, peer) in enumerate(chip_peers())
-    ]
+    late.swap()
+    late.over_y()
+    early.over_z()
     scatter.middle()
-    for copy in pieces:
-        copy.wait_recv()
-    total = half[chip].astype(F32)
-    for n in range(7):
-        total = total + piece_in[n].astype(F32)
-    done[c, chip] = total.astype(BF16)
-    spread = [links.start(done.at[c, chip], done.at[c, chip], peer) for _, peer in chip_peers()]
+    late.over_z()
+    early.spread()
+    late.spread()
     scatter.end()
-    out = exchange_out(links, s7, normed_out)
-    for copy in spread:
-        copy.wait_recv()
-    mirror = links.start(done.at[c], done.at[c], core_peer())
-    mirror.wait_recv()
-
-    def widen(k, carry):
-        weights_out[k] = done[k // 8, k % 8].astype(F32)
-        return carry
-
-    lax.fori_loop(0, 16, widen, 0)
+    out = exchange_out(links, s7, d_normed)
+    mixed = exchange_out(links, mixed_in, mixed_out)
+    early.mirror()
+    late.mirror()
     for copy in out:
         copy.wait_recv()
+    n_rows = skip[...].reshape(128, C).astype(F32) * rstd[...]
+    g_rows = d_normed[...].reshape(128, C).astype(F32) * gain[...]
+    mean = jnp.sum(g_rows * n_rows, axis=-1, keepdims=True) / C
+    d_skip = grad[...].reshape(128, C).astype(F32) + rstd[...] * (g_rows - n_rows * mean)
+    low, high = pl.ds(0, 128), pl.ds(128, 128)
+    even = (slope[low] * d_skip).astype(BF16)
+    odd = (slope[high] * d_skip).astype(BF16)
+    for p, block in enumerate((even, odd)):
+        rows = block.reshape(4, 32, C)
+        edges[0, p], edges[1, p] = rows[:, 0], rows[:, 31]
+    to_after = links.start(edges.at[1], halo.at[0], after)
+    to_before = links.start(edges.at[0], halo.at[1], before)
+    taps[2, low], taps[2, high] = even, odd
+    taps[1, low], taps[3, high] = odd, even
+    w_copy.wait()
+    to_after.wait_recv()
+    to_before.wait_recv()
+    first, last = slab > 0, slab < 127
+    even_before = shifted(even, halo[0, 0], False, first)
+    odd_before = shifted(odd, halo[0, 1], False, first)
+    even_after = shifted(even, halo[1, 0], True, last)
+    odd_after = shifted(odd, halo[1, 1], True, last)
+    taps[0, low], taps[0, high] = even_after, odd_after
+    taps[1, high], taps[3, low] = even_after, odd_before
+    taps[4, low], taps[4, high] = even_before, odd_before
+
+    def conv_tile(n, carry):
+        cut = pl.ds(pl.multiple_of(n * 256, 256), 256)
+        v = nt(taps[0], w_buf[0, cut])
+        for k in range(1, KW):
+            v = v + nt(taps[k], w_buf[k, cut])
+        grad_input[:, cut] = v.astype(BF16)
+        return carry
+
+    lax.fori_loop(0, 3, conv_tile, 0)
+    early.end()
+    late.end()
+    gw_out[0:DH] = a6[0].reshape(DH, C)
+    gwo_out[...] = a6[1].reshape(DH, C)
+    gw_out[DH : 3 * DH] = b6[...].reshape(2 * DH, C)
+    for copy in mixed:
+        copy.wait_recv()
     links.finish()
 
 
-def vmem_call(kernel, collective_id, inputs, outputs, scratch, limit, copies):
+def vmem_call(kernel, collective_id, inputs, outputs, scratch, limit, copies, hbm=0):
     spec = pl.BlockSpec(memory_space=VM)
+    far = pl.BlockSpec(memory_space=pl.ANY)
     return pl.pallas_call(
         kernel,
         out_shape=[jax.ShapeDtypeStruct(shape, dtype) for shape, dtype in outputs],
-        in_specs=[spec] * len(inputs),
+        in_specs=[spec] * (len(inputs) - hbm) + [far] * hbm,
         out_specs=[spec] * len(outputs),
         scratch_shapes=[pltpu.SemaphoreType.DMA((copies,)), pltpu.SemaphoreType.DMA((copies,))] + scratch,
         compiler_params=pltpu.CompilerParams(
@@ -484,50 +715,38 @@
     )(*inputs)
 
 
-def shift_halo(low_rows, high_rows):
-    forward = [(i, i + 1) for i in range(127)]
-    backward = [(target, source) for source, target in forward]
-    axes = ("seq", "head")
-    return lax.ppermute(high_rows, axes, forward), lax.ppermute(low_rows, axes, backward)
-
-
-def padded_2(block):
-    low, high = shift_halo(block[:, :2], block[:, -2:])
-    return jnp.concatenate([low, block, high], axis=1)
-
-
 def body(enc_in, conv_weight, norm_gain, w_qkv, w_out, grad_out):
-    enc = jnp.transpose(enc_in, (1, 0, 2))
+    enc = jnp.transpose(enc_in.reshape(32, 2, 4, 768), (1, 2, 0, 3))
+    edges = jnp.stack([enc_in[:2], enc_in[62:]])
     grad = jnp.transpose(grad_out, (1, 0, 2))
     w = jnp.transpose(w_qkv, (0, 2, 1)).reshape(3 * DH, C)
-    padded = padded_2(enc)
-    convolved = jnp.zeros((4, 64, C), F32)
-    for offset in range(KW):
-        convolved = convolved + jnp.einsum(
-            "bti,io->bto", padded[:, offset : offset + 64], conv_weight[offset], preferred_element_type=F32
-        )
-    activated, gelu_pull = jax.vjp(jax.nn.gelu, convolved)
-    skip = jnp.mean(activated.reshape(4, 32, 2, C), axis=2).astype(BF16)
-    skip_wide = skip.astype(F32)
-    inv_rms = lax.rsqrt(jnp.mean(skip_wide * skip_wide, axis=-1, keepdims=True) + 1e-06)
-    normed = (skip_wide * inv_rms * norm_gain).astype(BF16)
-
-    x_all, g_own, q, qt, kvt = vmem_call(
+    gain = norm_gain.reshape(1, C)
+    skip, rstd, slope, x_all, g_own, q, qt, kvt = vmem_call(
         gather_kernel,
         0,
-        [normed, grad, w],
+        [enc, edges, gain, grad, w, conv_weight],
         [
+            ((4, 32, C), BF16),
+            ((128, 1), F32),
+            ((256, C), F32),
             ((8, 4, 32, C), BF16),
             ((4, 32, C), BF16),
             ((4, 256, DH), BF16),
             ((DH, 1024), BF16),
             ((2 * DH, 1024), BF16),
         ],
-        [],
-        30,
-        16,
+        [
+            pltpu.SemaphoreType.DMA((6,)),
+            VM((6, KW, 768, 256), BF16),
+            VM((2, 2, 4, 768), BF16),
+            VM((KW, 256, 768), BF16),
+            VM((4, 32, C), BF16),
+        ],
+        45,
+        40,
+        1,
     )
-    head_sum, gwo, dq, dqt, dkv = vmem_call(
+    final, gwo, dq, dqt, dkv = vmem_call(
         attention_kernel,
         1,
         [g_own, q, qt, kvt, w_out],
@@ -558,51 +777,36 @@
             VM((3, 2 * DH, 1024), BF16),
             VM((8, 128, C), BF16),
         ]
-        + SCATTER_SCRATCH,
+        + SCATTER_SCRATCH[:-1],
         58,
-        36,
+        64,
     )
-    d_normed, weights = vmem_call(
+    mixed, gw, gwo, grad_input = vmem_call(
         gradient_kernel,
         2,
-        [x_all, dq, dqt, dkv, w, gwo],
-        [((4, 32, C), BF16), ((16, 48, C), F32)],
-        [VM((4, 256, 2 * DH), BF16), VM((8, 128, C), BF16)]
+        [x_all, dq, dqt, dkv, w, gwo, final, skip, rstd, gain, slope, grad, conv_weight],
+        [((4, 32, C), BF16), ((3 * DH, C), BF16), ((DH, C), BF16), ((256, 768), BF16)],
+        [pltpu.SemaphoreType.DMA, VM((4, 256, 2 * DH), BF16), VM((8, 128, C), BF16)]
         + SCATTER_SCRATCH
+        + SUM_SCRATCH * 2
         + [
-            VM((16, 48, C), BF16),
-            VM((8, 48, C), BF16),
-            VM((8, 48, C), BF16),
-            VM((7, 48, C), BF16),
-            VM((2, 8, 48, C), BF16),
+            VM((KW, 768, C), BF16),
+            VM((4, 32, C), BF16),
+            VM((2, 2, 4, C), BF16),
+            VM((2, 2, 4, C), BF16),
+            VM((KW, 256, C), BF16),
         ],
-        50,
-        40,
+        58,
+        48,
+        1,
     )
-    mixed = (skip_wide + head_sum.astype(F32)).astype(BF16)
-    d_normed = d_normed.astype(F32)
-    unit_rows = skip_wide * inv_rms
-    scaled = d_normed * norm_gain
-    d_skip = grad.astype(F32) + inv_rms * (
-        scaled - unit_rows * jnp.mean(scaled * unit_rows, axis=-1, keepdims=True)
-    )
-    d_act = jnp.repeat(d_skip, 2, axis=1) * 0.5
-    d_conv = gelu_pull(d_act)[0].astype(BF16)
-    d_pad = padded_2(d_conv)
-    grad_input = jnp.zeros((4, 64, enc_in.shape[2]), F32)
-    for offset in range(KW):
-        grad_input = grad_input + jnp.einsum(
-            "bto,io->bti",
-            d_pad[:, 4 - offset : 4 - offset + 64],
-            conv_weight[offset],
-            preferred_element_type=F32,
-        )
-    weights = weights.reshape(4 * DH, C)
+    mixed = (skip.astype(F32) + mixed.astype(F32)).astype(BF16)
+    grad_input = jnp.transpose(grad_input.reshape(2, 4, 32, 768), (2, 0, 1, 3)).reshape(64, 4, 768)
     return (
         jnp.transpose(mixed, (1, 0, 2)),
-        jnp.transpose(grad_input.astype(BF16), (1, 0, 2)),
-        jnp.transpose(weights[: 3 * DH].reshape(3, DH, C), (0, 2, 1)),
-        weights[3 * DH :],
+        grad_input,
+        jnp.transpose(gw.astype(F32).reshape(3, DH, C), (0, 2, 1)),
+        gwo.astype(F32),
     )
 
 

time: 261 us -> 198 us (0.76); the launches traced: 257 us -> 197 us
  matrix products: 21.5 us -> 0 us
  starting transfers between devices: 16.8 us -> 0 us
  Pallas kernels: 190 us -> 179 us
  local copies, waits for them, and re-layouts: 22.7 us -> 13 us
    dot_general x10 -> x0, matrix products: 21.5 us -> none  [the longest x5 13.8 us: body(): jnp.einsum('bti,io->bto', padded[:, offset:offset + 64], conv_weight[offs...]
    ppermute x4 -> x0, starting transfers between devices: 16.8 us -> none  [the longest x2 11 us: shift_halo(): lax.ppermute(low_rows, axes, backward)]
    pallas_call x3, Pallas kernels: 190 us -> 179 us  [vmem_call(): pl.pallas_call(kernel, out_shape=[jax.ShapeDtypeStruct(shape, dtype) for...]
    slice x4 -> x0, local copies, waits for them, and re-layouts: 6.75 us -> none  [the longest x1 4.18 us: body(): weights[:3 * DH].reshape(3, DH, C)]
    unnamed x38 -> x30, local copies, waits for them, and re-layouts: 13.4 us -> 9.28 us
    transpose x0 -> x2, other arithmetic: none -> 3.43 us  [the longest x1 2.26 us: body(): jnp.transpose(gw.astype(F32).reshape(3, DH, C), (0, 2, 1))]
  transfers between devices with their start and end apart: 4 -> 0, of which waited for: 1 -> 0; matrix products, arithmetic and copies ran while one was open for 7% -> 0% of each run, Pallas kernels for 0% -> 0%
where the time goes in v2:
time: 198 us; the launch traced here: 197 us
  Pallas kernels  179 us (90%)
  local copies, waits for them, and re-layouts  13 us (7%)
  other arithmetic  4.6 us (2%)
    pallas_call x3, Pallas kernels, vmem_call(): pl.pallas_call(kernel, out_shape=[jax.ShapeDtypeStruct(shape, dtype) for...  179 us
    unnamed x30, local copies, waits for them, and re-layouts  9.28 us

profile of v2, /device:TPU:1, one launch (start us, length us, event | category | flops | bytes accessed | tf_op | source)
XLA Modules:
  0.0 197.2 jit_solution(1094307549106261838)
XLA Ops:
  0.6 0.7 reshape.28.gain
  1.3 0.0 copy-start.10
  1.3 0.7 slice_bitcast_fusion.1
  2.1 1.1 copy.19
  3.2 0.0 copy-start.1
  3.2 1.2 copy.20
  4.4 0.0 copy-start
  4.4 1.5 copy-done
  5.9 52.3 %shard_map.93 = (bf16[4,32,1536]{2,1,0:T(8,128)(2,1)S(1)}, f32[128,1]{1,0:T(8,128)S(1)}, f32[256,1536]{1,0:T(8,128)S(1)}, bf16[8,4,32,1536]{3,2,1,0:T(8,128)(2,1...) custom-call(bf16[2,4,32,768]{3,2,1,0:T(8,128)(2,1)S(1)} %bitcast.28,, ...), custom_call_target="tpu_custom_call" | custom-call | tf_op jit(solution)/shard_map/pallas_call | solution.py:706
  58.2 0.0 copy-done.10
  58.2 0.0 copy-done.1
  58.2 0.0 copy-start.2
  58.2 1.1 copy-done.2
  59.4 0.0 copy-start.3
  59.4 0.7 copy-done.3
  60.1 0.0 copy-start.5
  60.1 0.9 copy-done.5
  61.0 0.0 copy-start.6
  61.0 0.8 copy-done.6
  61.8 0.0 copy-start.7
  61.8 0.7 copy-done.7
  62.6 0.0 copy-start.8
  62.6 0.7 copy-done.8
  63.3 0.0 copy-start.9
  63.3 0.6 copy-done.9
  63.9 61.6 %shard_map.94 = (bf16[4,32,1536]{2,1,0:T(8,128)(2,1)}, bf16[192,1536]{1,0:T(8,128)(2,1)}, bf16[4,256,192]{2,1,0:T(8,128)(2,1)}, bf16[192,1024]{1,0:T(8,128)(2,1)}, bf16[384,1024]{1,0:T(8,128)(2,1)}) custom-call(bf16[4,32,1536]{2,1,0:T(8,128)(2,1)} %copy-done.7, bf16[4,256,192]{2,1,0:T(8,128)(2,1)} %copy-done.6, bf16[192,1024]{1,0:T(8,128)(2,1)} %copy-done.8, ...), custom_call_target="tpu_custom_call" | custom-call | tf_op jit(solution)/shard_map/pallas_call | solution.py:706
  125.5 0.0 copy-start.4
  125.5 65.0 %shard_map.95 = (bf16[4,32,1536]{2,1,0:T(8,128)(2,1)}, bf16[576,1536]{1,0:T(8,128)(2,1)}, bf16[192,1536]{1,0:T(8,128)(2,1)}, bf16[256,768]{1,0:T(8,128)(2,1)}) custom-call(bf16[8,4,32,1536]{3,2,1,0:T(8,128)(2,1)} %get-tuple-element.22.x_all, bf16[4,256,192]{2,1,0:T(8,128)(2,1)} %get-tuple-element.27.dq, bf16[192,1024]{1,0:T(8,128)(2,1)} %get-tuple-element.28.dqt, ...), custom_call_target="tpu_custom_call" | custom-call | tf_op jit(solution)/shard_map/pallas_call | solution.py:706
  190.5 0.0 copy-start.13
  190.5 0.0 copy-start.12
  190.5 0.0 copy-done.4
  190.5 1.2 fusion
  191.7 0.0 copy-start.11
  191.7 1.1 copy.16
  192.8 0.0 copy-done.13
  192.8 1.1 copy.15
  193.8 0.0 copy-done.12
  193.8 1.1 convert_element_type.16
  195.0 0.0 copy-done.11
  195.0 2.3 %convert_bitcast_fusion = f32[3,1536,192]{1,2,0:T(8,128)} fusion(bf16[3,192,1536]{2,1,0:T(8,128)(2,1)S(1)} %bitcast.29), kind=kLoop, calls=%fused_computation | loop fusion | flops 884736 | bytes 5308416 | tf_op jit(solution)/shard_map/transpose | solution.py:808
  (1 shorter events, 0.0 us)
Async XLA Ops:
  1.3 56.9 %copy-start.10 = (f32[1,1536]{1,0:T(1,128)}, f32[1,1536]{1,0:T(1,128)S(1)}, u32[]{:S(2)}) copy-start(f32[1,1536]{1,0:T(1,128)S(1)} %reshape.28.gain) | copy-start | bytes 18436
  3.2 55.0 %copy-start.1 = (bf16[32,4,1536]{2,0,1:T(8,128)(2,1)}, bf16[32,4,1536]{2,0,1:T(8,128)(2,1)S(1)}, u32[]{:S(2)}) copy-start(bf16[32,4,1536]{2,0,1:T(8,128)(2,1)S(1)} %copy.19) | copy-start | bytes 1179652
  4.4 1.5 copy-start
  58.2 1.1 copy-start.2
  59.4 0.7 copy-start.3
  60.1 0.9 copy-start.5
  61.0 0.8 copy-start.6
  61.8 0.7 copy-start.7
  62.6 0.7 copy-start.8
  63.3 0.6 copy-start.9
  125.5 65.0 %copy-start.4 = (bf16[4,32,1536]{2,1,0:T(8,128)(2,1)S(1)}, bf16[4,32,1536]{2,1,0:T(8,128)(2,1)}, u32[]{:S(2)}) copy-start(bf16[4,32,1536]{2,1,0:T(8,128)(2,1)} %copy-done.3) | copy-start | bytes 1179652
  190.5 2.3 %copy-start.13 = (bf16[256,768]{1,0:T(8,128)(2,1)S(1)}, bf16[256,768]{1,0:T(8,128)(2,1)}, u32[]{:S(2)}) copy-start(bf16[256,768]{1,0:T(8,128)(2,1)} %get-tuple-element.35) | copy-start | bytes 1179652
  190.5 3.3 %copy-start.12 = (bf16[192,1536]{1,0:T(8,128)(2,1)S(1)}, bf16[192,1536]{1,0:T(8,128)(2,1)}, u32[]{:S(2)}) copy-start(bf16[192,1536]{1,0:T(8,128)(2,1)} %get-tuple-element.37) | copy-start | bytes 1769476
  191.7 3.3 %copy-start.11 = (bf16[576,1536]{1,0:T(8,128)(2,1)S(1)}, bf16[576,1536]{1,0:T(8,128)(2,1)}, u32[]{:S(2)}) copy-start(bf16[576,1536]{1,0:T(8,128)(2,1)} %get-tuple-element.36) | copy-start | bytes 5308420

commit v3 on v2

--- a/solution.py
+++ b/solution.py
@@ -135,51 +135,63 @@
     def forward(self):
         up, down = x_neighbours()
         z, zl, other = zl_peer(), self.zl, 1 - self.zl
-        self.rest = []
 
         def send(part, peer):
             return self.links.start(part, part, peer)
 
         self.up[0].wait_recv()
         self.relay_0 = send(self.at(zl, 3, 0), up)
-        self.rest.append(send(self.at(zl, 3, 0), z))
+        self.low_0 = send(self.at(zl, 3, 0), z)
         self.down[1].wait_recv()
         self.relay_1 = send(self.at(zl, 1, 1), down)
-        self.rest.append(send(self.at(zl, 1, 1), z))
+        self.high_1 = send(self.at(zl, 1, 1), z)
         self.z[2].wait_recv()
-        self.over_2 = send(self.at(other, 0, 2), up)
-        self.rest.append(send(self.at(other, 0, 2), down))
+        self.low_2 = send(self.at(other, 0, 2), up)
+        self.high_2 = send(self.at(other, 0, 2), down)
         self.z[3].wait_recv()
-        self.over_3 = send(self.at(other, 0, 3), down)
-        self.rest.append(send(self.at(other, 0, 3), up))
+        self.high_3 = send(self.at(other, 0, 3), down)
+        self.low_3 = send(self.at(other, 0, 3), up)
         self.down[0].wait_recv()
-        self.rest.append(send(self.at(zl, 1, 0), z))
+        self.high_0 = send(self.at(zl, 1, 0), z)
         self.up[1].wait_recv()
-        self.rest.append(send(self.at(zl, 3, 1), z))
+        self.low_1 = send(self.at(zl, 3, 1), z)
         self.up[2].wait_recv()
-        self.rest.append(send(self.at(zl, 3, 2), up))
+        self.relay_2 = send(self.at(zl, 3, 2), up)
         self.down[3].wait_recv()
-        self.rest.append(send(self.at(zl, 1, 3), down))
+        self.relay_3 = send(self.at(zl, 1, 3), down)
 
     def relay(self):
         up, down = x_neighbours()
         z, zl, other = zl_peer(), self.zl, 1 - self.zl
 
         def send(part, peer):
-            self.rest.append(self.links.start(part, part, peer))
+            return self.links.start(part, part, peer)
 
         self.relay_0.wait_recv()
-        send(self.at(zl, 2, 0), z)
+        self.far_0 = send(self.at(zl, 2, 0), z)
         self.relay_1.wait_recv()
-        send(self.at(zl, 2, 1), z)
-        self.over_2.wait_recv()
-        send(self.at(other, 3, 2), up)
-        self.over_3.wait_recv()
-        send(self.at(other, 1, 3), down)
+        self.far_1 = send(self.at(zl, 2, 1), z)
+        self.low_2.wait_recv()
+        self.far_2 = send(self.at(other, 3, 2), up)
+        self.high_3.wait_recv()
+        self.far_3 = send(self.at(other, 1, 3), down)
+
+    def steps(self):
+        other = 1 - self.zl
+        return [
+            (self.zl, 3, [self.up[3]]),
+            (self.zl, 1, [self.down[2]]),
+            (other, 0, [self.z[0], self.z[1]]),
+            (self.zl, 2, [self.relay_2, self.relay_3]),
+            (other, 3, [self.low_0, self.low_1, self.low_3]),
+            (other, 1, [self.high_0, self.high_1, self.high_2]),
+            (other, 2, [self.far_0, self.far_1, self.far_2, self.far_3]),
+        ]
 
     def end(self):
-        for copy in self.rest + [self.up[3], self.down[2], self.z[0], self.z[1]]:
-            copy.wait_recv()
+        for _, _, copies in self.steps():
+            for copy in copies:
+                copy.wait_recv()
 
 
 def exchange_in(links, slab, buf, me):
@@ -295,10 +307,12 @@
     return jnp.where(place == 0, fill, pltpu.roll(wide, 1, 0)).astype(BF16)
 
 
-def gather_kernel(
-    enc, edges, gain, grad, w, conv_w,
-    skip, rstd, slope, x_all, g_own, q, qt, kvt,
+def attention_kernel(
+    enc, edges, gain, grad, w, w_out, conv_w,
+    skip, rstd, slope, x_all, mixed_out, gwo, dq_out, dqt_out, dkv_out,
     send, recv, w_sem, w_buf, halo, taps, normed,
+    g_all, q, qt, kv, peak, chunk_peak, total, o_acc, e_all, ob, ot, do, dot_, delta,
+    ds, dq_acc, acc, dkv_send, dkv_recv, terms, s1, s2, s3, s4, s5, s6,
 ):
     y, zh, c, zl, x = coords()
     me = zl * 4 + x
@@ -307,15 +321,21 @@
 
     def tile_copy(n):
         cut = pl.ds(pl.multiple_of(n * 256, 256), 256)
-        return pltpu.make_async_copy(conv_w.at[:, :, cut], w_buf.at[n], w_sem.at[n])
-
-    for n in range(6):
+        return pltpu.make_async_copy(conv_w.at[:, :, cut], w_buf.at[n % 3], w_sem.at[n % 3])
+
+    for n in range(3):
         tile_copy(n).start()
-    met(greet([*x_neighbours(), zl_peer(), after, before] + [peer for _, peer in group_peers()]))
+    met(
+        greet(
+            x_peers()
+            + [zl_peer(), core_peer(), y_pair_peer(), after, before]
+            + [peer for _, peer in group_peers()]
+        )
+    )
     links = Links(send, recv)
     to_after = links.start(edges.at[1], halo.at[0], after)
     to_before = links.start(edges.at[0], halo.at[1], before)
-    mine = group()
+    grad_copies = exchange_in(links, grad, g_all, me)
     even, odd = enc[0].reshape(128, 768), enc[1].reshape(128, 768)
     low, high = pl.ds(0, 128), pl.ds(128, 128)
     taps[2, low], taps[2, high] = even, odd
@@ -335,9 +355,14 @@
     def conv_tile(n, squares):
         tile_copy(n).wait()
         cut = pl.ds(pl.multiple_of(n * 256, 256), 256)
-        v = nn(taps[0], w_buf[n, 0])
+        v = nn(taps[0], w_buf[n % 3, 0])
         for k in range(1, KW):
-            v = v + nn(taps[k], w_buf[n, k])
+            v = v + nn(taps[k], w_buf[n % 3, k])
+
+        @pl.when(n < 3)
+        def _():
+            tile_copy(n + 3).start()
+
         v2 = v * v
         t = jnp.tanh(root * v * (1.0 + 0.044715 * v2))
         half = 0.5 * (1.0 + t)
@@ -357,44 +382,40 @@
     copies = exchange_in(links, normed, x_all, me)
     gather = Gather(links, x_all)
     gather.begin(copies)
-    g_own[mine] = grad[mine]
-    copies = [links.start(grad.at[g], g_own.at[mine], peer) for g, peer in group_peers()]
+    kv_core, kv_pair = [], []
+
+    def project(k):
+        rows = x_all[k].reshape(128, C)
+        part = nt(rows, w[0:DH])
+        q[k // 2, pl.ds((k % 2) * 128, 128)] = part.astype(BF16)
+        cut = pl.ds(pl.multiple_of(k * 128, 128), 128)
+        qt[:, cut] = jnp.transpose(part).astype(BF16)
+        kv[0, :, cut] = nt(w[DH : 3 * DH], rows).astype(BF16)
+        kv_pair.append((cut, links.start(kv.at[0, :, cut], kv.at[2, :, cut], y_pair_peer())))
+        kv_core.append(links.start(kv.at[0, :, cut], kv.at[1, :, cut], core_peer()))
+
+    project(me)
     gather.forward()
+    for copy in grad_copies:
+        copy.wait_recv()
+    late = Gather(links, g_all)
+    late.begin(None)
+    gather.up[3].wait_recv()
+    project(zl * 4 + (x + 3) % 4)
     gather.relay()
-    gather.end()
-
-    def project(i, carry):
-        rows = rows_of(x_all, i)
-        part = nt(rows, w[0:DH])
-        q[i] = part.astype(BF16)
-        columns = pl.ds(pl.multiple_of(i * 256, 256), 256)
-        qt[:, columns] = jnp.transpose(part).astype(BF16)
-        kvt[:, columns] = nt(w[DH : 3 * DH], rows).astype(BF16)
-        return carry
-
-    lax.fori_loop(0, 4, project, 0)
-    for copy in copies:
-        copy.wait_recv()
-    links.finish()
-
-
-def attention_kernel(
-    g_own, q, qt, kvt, w_out,
-    mixed_out, gwo, dq_out, dqt_out, dkv_out,
-    send, recv, g_all, kv, peak, chunk_peak, total, o_acc, e_all, ob, ot, do, dot_, delta,
-    ds, dq_acc, acc, dkv_send, dkv_recv, terms, s1, s2, s3, s4, s5, s6,
-):
-    y, zh, c, zl, x = coords()
-    me = zl * 4 + x
-    met(greet(x_peers() + [zl_peer(), core_peer(), y_pair_peer()]))
-    links = Links(send, recv)
-    kv[0] = kvt[...]
-    to_pair = links.start(kvt, kv.at[2], y_pair_peer())
-    to_core = links.start(kvt, kv.at[1], core_peer())
-    g_all[me] = g_own[...]
-    gather = Gather(links, g_all)
-    gather.begin(None)
-
+    for n, (plane, dx, waits) in enumerate(gather.steps()):
+        if n > 0:
+            for copy in waits:
+                copy.wait_recv()
+            project(plane * 4 + (x + dx) % 4)
+    kv_relay = []
+
+    def pass_on(first, last):
+        for cut, copy in kv_pair[first:last]:
+            copy.wait_recv()
+            kv_relay.append(links.start(kv.at[2, :, cut], kv.at[3, :, cut], core_peer()))
+
+    pass_on(0, 6)
     peak[...] = jnp.full_like(peak, -jnp.inf)
     total[...] = jnp.zeros_like(total)
     o_acc[...] = jnp.zeros_like(o_acc)
@@ -418,14 +439,15 @@
         lax.fori_loop(0, 4, tile, 0, unroll=True)
 
     forward(0)
-    to_core.wait_recv()
+    pass_on(6, 8)
+    for copy in kv_core:
+        copy.wait_recv()
+    late.forward()
     forward(1)
-    gather.forward()
-    to_pair.wait_recv()
-    relay = links.start(kv.at[2], kv.at[3], core_peer())
-    gather.relay()
+    late.relay()
     forward(2)
-    relay.wait_recv()
+    for copy in kv_relay:
+        copy.wait_recv()
     forward(3)
 
     def finish_tile(i, carry):
@@ -442,7 +464,7 @@
 
     lax.fori_loop(0, 4, finish_tile, 0)
     scatter = Scatter(links, terms, s1, s2, s3, s4, s5, s6, mixed_out)
-    gather.end()
+    late.end()
     scatter.begin_other()
     scatter.begin_own()
 
@@ -721,36 +743,15 @@
     grad = jnp.transpose(grad_out, (1, 0, 2))
     w = jnp.transpose(w_qkv, (0, 2, 1)).reshape(3 * DH, C)
     gain = norm_gain.reshape(1, C)
-    skip, rstd, slope, x_all, g_own, q, qt, kvt = vmem_call(
-        gather_kernel,
+    skip, rstd, slope, x_all, final, gwo, dq, dqt, dkv = vmem_call(
+        attention_kernel,
         0,
-        [enc, edges, gain, grad, w, conv_weight],
+        [enc, edges, gain, grad, w, w_out, conv_weight],
         [
             ((4, 32, C), BF16),
             ((128, 1), F32),
             ((256, C), F32),
             ((8, 4, 32, C), BF16),
-            ((4, 32, C), BF16),
-            ((4, 256, DH), BF16),
-            ((DH, 1024), BF16),
-            ((2 * DH, 1024), BF16),
-        ],
-        [
-            pltpu.SemaphoreType.DMA((6,)),
-            VM((6, KW, 768, 256), BF16),
-            VM((2, 2, 4, 768), BF16),
-            VM((KW, 256, 768), BF16),
-            VM((4, 32, C), BF16),
-        ],
-        45,
-        40,
-        1,
-    )
-    final, gwo, dq, dqt, dkv = vmem_call(
-        attention_kernel,
-        1,
-        [g_own, q, qt, kvt, w_out],
-        [
             ((4, 32, C), BF16),
             ((DH, C), BF16),
             ((4, 256, DH), BF16),
@@ -758,7 +759,14 @@
             ((2 * DH, 1024), BF16),
         ],
         [
+            pltpu.SemaphoreType.DMA((3,)),
+            VM((3, KW, 768, 256), BF16),
+            VM((2, 2, 4, 768), BF16),
+            VM((KW, 256, 768), BF16),
+            VM((4, 32, C), BF16),
             VM((8, 4, 32, C), BF16),
+            VM((4, 256, DH), BF16),
+            VM((DH, 1024), BF16),
             VM((4, 2 * DH, 1024), BF16),
             VM((4, 256, 1), F32),
             VM((4, 4, 256, 1), F32),
@@ -778,12 +786,13 @@
             VM((8, 128, C), BF16),
         ]
         + SCATTER_SCRATCH[:-1],
-        58,
-        64,
+        61,
+        120,
+        1,
     )
     mixed, gw, gwo, grad_input = vmem_call(
         gradient_kernel,
-        2,
+        1,
         [x_all, dq, dqt, dkv, w, gwo, final, skip, rstd, gain, slope, grad, conv_weight],
         [((4, 32, C), BF16), ((3 * DH, C), BF16), ((DH, C), BF16), ((256, 768), BF16)],
         [pltpu.SemaphoreType.DMA, VM((4, 256, 2 * DH), BF16), VM((8, 128, C), BF16)]

time: 198 us -> 190 us (0.960)
  local copies, waits for them, and re-layouts: 13 us -> 7.76 us
  Pallas kernels: 179 us -> 176 us
    unnamed x30 -> x10, local copies, waits for them, and re-layouts: 9.28 us -> 2.88 us
    pallas_call x3 -> x2, Pallas kernels: 179 us -> 176 us  [vmem_call(): pl.pallas_call(kernel, out_shape=[jax.ShapeDtypeStruct(shape, dtype) for...]
where the time goes in v3:
time: 190 us; the launch traced here: 189 us
  Pallas kernels  176 us (93%)
  local copies, waits for them, and re-layouts  7.76 us (4%)
  other arithmetic  5.2 us (3%)
    pallas_call x2, Pallas kernels, vmem_call(): pl.pallas_call(kernel, out_shape=[jax.ShapeDtypeStruct(shape, dtype) for...  176 us

profile of v3, /device:TPU:1, one launch (start us, length us, event | category | flops | bytes accessed | tf_op | source)
XLA Modules:
  0.0 189.2 jit_solution(16947804873943693254)
XLA Ops:
  0.6 1.3 reshape.28.gain
  1.9 0.7 slice_bitcast_fusion.1
  2.7 0.6 pad_maximum_fusion.edges
  3.3 1.8 copy.19
  5.1 1.8 copy.20
  6.9 107.0 %shard_map.93 = (bf16[4,32,1536]{2,1,0:T(8,128)(2,1)}, f32[128,1]{1,0:T(8,128)}, f32[256,1536]{1,0:T(8,128)}, bf16[8,4,32,1536]{3,2,1,0:T(8,128)(2,1)}, bf16[4,3...) custom-call(bf16[2,4,32,768]{3,2,1,0:T(8,128)(2,1)} %bitcast.29, ...), custom_call_target="tpu_custom_call" | custom-call | tf_op jit(solution)/shard_map/pallas_call | solution.py:728
  113.9 0.0 copy-start.1
  113.9 68.5 %shard_map.94 = (bf16[4,32,1536]{2,1,0:T(8,128)(2,1)}, bf16[576,1536]{1,0:T(8,128)(2,1)}, bf16[192,1536]{1,0:T(8,128)(2,1)}, bf16[256,768]{1,0:T(8,128)(2,1)}) custom-call(bf16[8,4,32,1536]{3,2,1,0:T(8,128)(2,1)} %get-tuple-element.18.x_all, bf16[4,256,192]{2,1,0:T(8,128)(2,1)} %get-tuple-element.19.dq, bf16[192,1024]{1,0:T(8,128)(2,1)} %get-tuple-element.20.dqt, ...), custom_call_target="tpu_custom_call" | custom-call | tf_op jit(solution)/shard_map/pallas_call | solution.py:728
  182.5 0.0 copy-start.3
  182.5 0.0 copy-start.2
  182.5 0.0 copy-done.1
  182.5 1.2 fusion
  183.7 0.0 copy-start
  183.7 1.1 copy.16
  184.8 0.0 copy-done.3
  184.8 1.1 copy.15
  185.8 0.0 copy-done.2
  185.8 1.1 convert_element_type.16
  187.0 0.0 copy-done
  187.0 2.3 %convert_bitcast_fusion = f32[3,1536,192]{1,2,0:T(8,128)} fusion(bf16[3,192,1536]{2,1,0:T(8,128)(2,1)S(1)} %bitcast.28), kind=kLoop, calls=%fused_computation | loop fusion | flops 884736 | bytes 5308416 | tf_op jit(solution)/shard_map/transpose | solution.py:817
Async XLA Ops:
  113.9 68.6 %copy-start.1 = (bf16[4,32,1536]{2,1,0:T(8,128)(2,1)S(1)}, bf16[4,32,1536]{2,1,0:T(8,128)(2,1)}, u32[]{:S(2)}) copy-start(bf16[4,32,1536]{2,1,0:T(8,128)(2,1)} %get-tuple-element.17.skip) | copy-start | bytes 1179652
  182.5 2.3 %copy-start.3 = (bf16[256,768]{1,0:T(8,128)(2,1)S(1)}, bf16[256,768]{1,0:T(8,128)(2,1)}, u32[]{:S(2)}) copy-start(bf16[256,768]{1,0:T(8,128)(2,1)} %get-tuple-element.27) | copy-start | bytes 1179652
  182.5 3.3 %copy-start.2 = (bf16[192,1536]{1,0:T(8,128)(2,1)S(1)}, bf16[192,1536]{1,0:T(8,128)(2,1)}, u32[]{:S(2)}) copy-start(bf16[192,1536]{1,0:T(8,128)(2,1)} %get-tuple-element.29) | copy-start | bytes 1769476
  183.7 3.3 %copy-start = (bf16[576,1536]{1,0:T(8,128)(2,1)S(1)}, bf16[576,1536]{1,0:T(8,128)(2,1)}, u32[]{:S(2)}) copy-start(bf16[576,1536]{1,0:T(8,128)(2,1)} %get-tuple-element.28) | copy-start | bytes 5308420

commit v4 on v3

--- a/solution.py
+++ b/solution.py
@@ -208,11 +208,14 @@
         y, zh, c, zl, x = coords()
         self.zl, self.x = zl, x
         self.me = zl * 4 + x
+        self.other_half, self.own_half = 1 - y // 2, y // 2
+        self.low = pl.ds(pl.multiple_of(self.other_half * 64, 64), 64)
+        self.high = pl.ds(pl.multiple_of(self.own_half * 64, 64), 64)
 
     def begin_other(self):
         zl, x, links = self.zl, self.x, self.links
         other = 1 - zl
-        low, high = pl.ds(0, 64), pl.ds(64, 64)
+        low, high = self.low, self.high
         self.c_pair = [
             links.start(self.terms.at[other * 4 + k, high], self.pair.at[k], zl_peer()) for k in range(4)
         ]
@@ -223,7 +226,7 @@
 
     def begin_own(self):
         zl, x, links = self.zl, self.x, self.links
-        low = pl.ds(0, 64)
+        low = self.low
         self.c_first = [
             links.start(self.terms.at[zl * 4 + (x + d) % 4, low], self.first.at[d - 1], peer)
             for d, peer in zip((1, 2, 3), x_peers())
@@ -231,7 +234,7 @@
 
     def middle(self):
         zl, x, links = self.zl, self.x, self.links
-        low, high = pl.ds(0, 64), pl.ds(64, 64)
+        low, high = self.low, self.high
         for copy in self.c_pair:
             copy.wait_recv()
 
@@ -254,19 +257,21 @@
         self.second[3] = total.astype(BF16)
         self.c_last = links.start(self.second.at[3], self.last, zl_peer())
 
-    def end(self):
-        zl, x = self.zl, self.x
-        low = pl.ds(0, 64)
-        for copy in self.c_first + self.c_third + [self.c_last]:
+    def end_low(self):
+        for copy in self.c_first + [self.c_last]:
             copy.wait_recv()
-        total = self.terms[self.me, low].astype(F32) + self.last[...].astype(F32)
+        total = self.terms[self.me, self.low].astype(F32) + self.last[...].astype(F32)
         for k in range(3):
             total = total + self.first[k].astype(F32)
-        self.final[0:2] = total.astype(BF16).reshape(2, 32, C)
-        total = self.pair_sum[x].astype(F32)
+        self.final[pl.ds(self.other_half * 2, 2)] = total.astype(BF16).reshape(2, 32, C)
+
+    def end_high(self):
+        for copy in self.c_third:
+            copy.wait_recv()
+        total = self.pair_sum[self.x].astype(F32)
         for k in range(3):
             total = total + self.third[k].astype(F32)
-        self.final[2:4] = total.astype(BF16).reshape(2, 32, C)
+        self.final[pl.ds(self.own_half * 2, 2)] = total.astype(BF16).reshape(2, 32, C)
 
 
 SCATTER_SCRATCH = [
@@ -527,7 +532,8 @@
         return carry
 
     lax.fori_loop(0, 3, w_out_gradient, 0)
-    scatter.end()
+    scatter.end_low()
+    scatter.end_high()
     near.wait_recv()
     pair.wait_recv()
     dkv_out[...] = (acc[...] + dkv_recv[1].astype(F32) + dkv_recv[2].astype(F32)).astype(BF16)
@@ -667,16 +673,20 @@
     late.over_y()
     early.over_z()
     scatter.middle()
+    early.spread()
+    mine = group()
+    scatter.end_low()
+    near, *others = group_peers()
+    out = [links.start(s7.at[g], d_normed.at[mine], peer) for g, peer in others]
     late.over_z()
-    early.spread()
+    scatter.end_high()
+    out.append(links.start(s7.at[near[0]], d_normed.at[mine], near[1]))
+    d_normed[mine] = s7[mine]
     late.spread()
-    scatter.end()
-    out = exchange_out(links, s7, d_normed)
-    mixed = exchange_out(links, mixed_in, mixed_out)
     early.mirror()
-    late.mirror()
     for copy in out:
         copy.wait_recv()
+    mixed = exchange_out(links, mixed_in, mixed_out)
     n_rows = skip[...].reshape(128, C).astype(F32) * rstd[...]
     g_rows = d_normed[...].reshape(128, C).astype(F32) * gain[...]
     mean = jnp.sum(g_rows * n_rows, axis=-1, keepdims=True) / C
@@ -689,6 +699,7 @@
         edges[0, p], edges[1, p] = rows[:, 0], rows[:, 31]
     to_after = links.start(edges.at[1], halo.at[0], after)
     to_before = links.start(edges.at[0], halo.at[1], before)
+    late.mirror()
     taps[2, low], taps[2, high] = even, odd
     taps[1, low], taps[3, high] = odd, even
     w_copy.wait()

time: 190 us -> 181 us (0.953)
  Pallas kernels: 176 us -> 166 us
    pallas_call x2, Pallas kernels: 176 us -> 166 us  [vmem_call(): pl.pallas_call(kernel, out_shape=[jax.ShapeDtypeStruct(shape, dtype) for...]
where the time goes in v4:
time: 181 us; the launch traced here: 180 us
  Pallas kernels  166 us (92%)
  local copies, waits for them, and re-layouts  7.76 us (4%)
  other arithmetic  5.2 us (3%)
    pallas_call x2, Pallas kernels, vmem_call(): pl.pallas_call(kernel, out_shape=[jax.ShapeDtypeStruct(shape, dtype) for...  166 us

profile of v4, /device:TPU:1, one launch (start us, length us, event | category | flops | bytes accessed | tf_op | source)
XLA Modules:
  0.0 179.7 jit_solution(4203199958595674208)
XLA Ops:
  0.6 1.3 reshape.28.gain
  1.9 0.7 slice_bitcast_fusion.1
  2.7 0.6 pad_maximum_fusion.edges
  3.3 1.8 %copy.19 = bf16[32,4,1536]{2,0,1:T(8,128)(2,1)} copy(bf16[32,4,1536]{2,1,0:T(4,128)(2,1)} %param.11) | data formatting | bytes 786432 | tf_op args[5]
  5.1 1.8 %copy.20 = bf16[32,2,4,768]{3,0,2,1:T(8,128)(2,1)} copy(bf16[32,2,4,768]{3,2,1,0:T(4,128)(2,1)} %bitcast.30) | data formatting | bytes 786432 | tf_op jit(solution)/shard_map/reshape | solution.py:752
  6.9 107.0 %shard_map.93 = (bf16[4,32,1536]{2,1,0:T(8,128)(2,1)}, f32[128,1]{1,0:T(8,128)}, f32[256,1536]{1,0:T(8,128)}, bf16[8,4,32,1536]{3,2,1,0:T(8,128)(2,1)}, bf16[4,3...) custom-call(bf16[2,4,32,768]{3,2,1,0:T(8,128)(2,1)} %bitcast.29, ...), custom_call_target="tpu_custom_call" | custom-call | tf_op jit(solution)/shard_map/pallas_call | solution.py:739
  113.9 0.0 copy-start.1
  113.9 59.0 %shard_map.94 = (bf16[4,32,1536]{2,1,0:T(8,128)(2,1)}, bf16[576,1536]{1,0:T(8,128)(2,1)}, bf16[192,1536]{1,0:T(8,128)(2,1)}, bf16[256,768]{1,0:T(8,128)(2,1)}) custom-call(bf16[8,4,32,1536]{3,2,1,0:T(8,128)(2,1)} %get-tuple-element.18.x_all, bf16[4,256,192]{2,1,0:T(8,128)(2,1)} %get-tuple-element.19.dq, bf16[192,1024]{1,0:T(8,128)(2,1)} %get-tuple-element.20.dqt, ...), custom_call_target="tpu_custom_call" | custom-call | tf_op jit(solution)/shard_map/pallas_call | solution.py:739
  173.0 0.0 copy-start.3
  173.0 0.0 copy-start.2
  173.0 0.0 copy-done.1
  173.0 1.2 fusion
  174.2 0.0 copy-start
  174.2 1.1 copy.16
  175.3 0.0 copy-done.3
  175.3 1.1 copy.15
  176.3 0.0 copy-done.2
  176.3 1.1 convert_element_type.16
  177.5 0.0 copy-done
  177.5 2.3 %convert_bitcast_fusion = f32[3,1536,192]{1,2,0:T(8,128)} fusion(bf16[3,192,1536]{2,1,0:T(8,128)(2,1)S(1)} %bitcast.28), kind=kLoop, calls=%fused_computation | loop fusion | flops 884736 | bytes 5308416 | tf_op jit(solution)/shard_map/transpose | solution.py:828
Async XLA Ops:
  113.9 59.1 %copy-start.1 = (bf16[4,32,1536]{2,1,0:T(8,128)(2,1)S(1)}, bf16[4,32,1536]{2,1,0:T(8,128)(2,1)}, u32[]{:S(2)}) copy-start(bf16[4,32,1536]{2,1,0:T(8,128)(2,1)} %get-tuple-element.17.skip) | copy-start | bytes 1179652
  173.0 2.3 %copy-start.3 = (bf16[256,768]{1,0:T(8,128)(2,1)S(1)}, bf16[256,768]{1,0:T(8,128)(2,1)}, u32[]{:S(2)}) copy-start(bf16[256,768]{1,0:T(8,128)(2,1)} %get-tuple-element.27) | copy-start | bytes 1179652
  173.0 3.3 %copy-start.2 = (bf16[192,1536]{1,0:T(8,128)(2,1)S(1)}, bf16[192,1536]{1,0:T(8,128)(2,1)}, u32[]{:S(2)}) copy-start(bf16[192,1536]{1,0:T(8,128)(2,1)} %get-tuple-element.29) | copy-start | bytes 1769476
  174.2 3.3 %copy-start = (bf16[576,1536]{1,0:T(8,128)(2,1)S(1)}, bf16[576,1536]{1,0:T(8,128)(2,1)}, u32[]{:S(2)}) copy-start(bf16[576,1536]{1,0:T(8,128)(2,1)} %get-tuple-element.28) | copy-start | bytes 5308420
